TPU v7x, 32 devices: a whole 2x2x4 slice. The times are simulated.
32 devices in a mesh: fsdp: 16 (over z, y, x), seq: 2 (over core).
Axes of the slice: x: 2, y: 2, z: 4, core: 2. Of those that a mesh axis runs over, the one named last changes fastest.
Arguments:
- hidden_in: bfloat16 [16, 512, 768], P('fsdp', 'seq'), may hold values from -6 to 6
- query_weight: bfloat16 [768, 768], P(('fsdp', 'seq')), may hold values from -0.21875 to 0.21875
- query_bias: bfloat16 [768], P(('fsdp', 'seq')), may hold values from -3 to 3
- key_weight: bfloat16 [768, 768], P(('fsdp', 'seq')), may hold values from -0.21875 to 0.21875
- value_weight: bfloat16 [768, 768], P(('fsdp', 'seq')), may hold values from -0.21875 to 0.21875
- value_bias: bfloat16 [768], P(('fsdp', 'seq')), may hold values from -3 to 3
- output_weight: bfloat16 [768, 768], P(('fsdp', 'seq')), may hold values from -0.625 to 0.625
- output_bias: bfloat16 [768], P(('fsdp', 'seq')), may hold values from -3 to 3
- first_gain: bfloat16 [768], P(('fsdp', 'seq')), may hold values from 0.5 to 1.5
- first_shift: bfloat16 [768], P(('fsdp', 'seq')), may hold values from -3 to 3
- inner_weight: bfloat16 [768, 3072], P(('fsdp', 'seq')), may hold values from -0.21875 to 0.21875
- inner_bias: bfloat16 [3072], P(('fsdp', 'seq')), may hold values from -3 to 3
- outer_weight: bfloat16 [3072, 768], P(('fsdp', 'seq')), may hold values from -0.109375 to 0.109375
- outer_bias: bfloat16 [768], P(('fsdp', 'seq')), may hold values from -3 to 3
- second_gain: bfloat16 [768], P(('fsdp', 'seq')), may hold values from 0.5 to 1.5
- second_shift: bfloat16 [768], P(('fsdp', 'seq')), may hold values from -3 to 3
- relative_table: bfloat16 [512, 768], P(None, ('fsdp', 'seq')), may hold values from -6 to 6
- segments: int32 [16, 512], P('fsdp'), may hold values from 0 to 15, never falling along the last dimension, each value on 1 to 256 neighbouring positions
- buckets: int32 [1023], replicated, may hold values from 0 to 511
- predicted: int32 [16, 512], P('fsdp', 'seq'), may hold values 0 or 1
- labels: int32 [16, 512], P('fsdp', 'seq'), may hold values 0 or 1
- cotangent: bfloat16 [16, 512, 768], P('fsdp', 'seq'), may hold values from -6 to 6
Outputs:
- result: bfloat16 [16, 512, 768], P('fsdp', 'seq')
- input_grad: bfloat16 [16, 512, 768], P('fsdp', 'seq')
- query_weight_grad: float32 [768, 768], P(('fsdp', 'seq'))
- query_bias_grad: float32 [768], P(('fsdp', 'seq'))
- key_weight_grad: float32 [768, 768], P(('fsdp', 'seq'))
- value_weight_grad: float32 [768, 768], P(('fsdp', 'seq'))
- value_bias_grad: float32 [768], P(('fsdp', 'seq'))
- output_weight_grad: float32 [768, 768], P(('fsdp', 'seq'))
- output_bias_grad: float32 [768], P(('fsdp', 'seq'))
- first_gain_grad: float32 [768], P(('fsdp', 'seq'))
- first_shift_grad: float32 [768], P(('fsdp', 'seq'))
- inner_weight_grad: float32 [768, 3072], P(('fsdp', 'seq'))
- inner_bias_grad: float32 [3072], P(('fsdp', 'seq'))
- outer_weight_grad: float32 [3072, 768], P(('fsdp', 'seq'))
- outer_bias_grad: float32 [768], P(('fsdp', 'seq'))
- second_gain_grad: float32 [768], P(('fsdp', 'seq'))
- second_shift_grad: float32 [768], P(('fsdp', 'seq'))
- relative_table_grad: float32 [512, 768], P(None, ('fsdp', 'seq'))
- correct_count: int32 [], replicated
Inputs may be any that keep to these rules, and one draw needn't show every extreme that they name: `segments`: segment numbers never fall along a row; a document has at most 256 tokens. `buckets`: entry d is the bucket of relative distance d - 511.
All inputs are finite; a program needn't handle non-finite values. No bound on the sum of `predicted` or of `labels` on one device may be relied on, other than what follows from the above.
Results may differ from a plain program's by a relative error of at most 0.015.
Values may be sent and summed in bfloat16 or wider, within the bound.
A program may use at most 192 MiB of HBM per device.

v0:
```python
from functools import partial

import jax
import jax.numpy as jnp
from jax import lax
from jax.sharding import PartitionSpec as P

HEAD = 64


EPSILON = 1e-07
NEGATIVE = -1e30


def matmul(spec, left, right):
    return jnp.einsum(spec, left, right, preferred_element_type=jnp.float32)


def precise(spec, left, right):
    return jnp.einsum(spec, left, right, precision=lax.Precision.HIGHEST)


def skew_rows(scores_in, offset, columns):
    leading = scores_in.shape[:-2]
    row_count = scores_in.shape[-2]
    breadth = scores_in.shape[-1]
    flattened = scores_in.reshape(leading + (row_count * breadth,))
    flattened = jnp.concatenate(
        [flattened, jnp.zeros(leading + (2 * breadth,), scores_in.dtype)], axis=-1
    )
    selected = lax.dynamic_slice_in_dim(flattened, offset, row_count * (breadth - 1), len(leading))
    return selected.reshape(leading + (row_count, breadth - 1))[..., :columns]


def unskew_rows(values, offset, breadth):
    leading = values.shape[:-2]
    row_count = values.shape[-2]
    columns = values.shape[-1]
    padded = jnp.concatenate(
        [values, jnp.zeros(leading + (row_count, breadth - 1 - columns), values.dtype)], axis=-1
    )
    flattened = padded.reshape(leading + (row_count * (breadth - 1),))
    zero_room = jnp.zeros(leading + (row_count * breadth + 2 * breadth,), values.dtype)
    placed = lax.dynamic_update_slice_in_dim(zero_room, flattened, offset, len(leading))
    return placed[..., : row_count * breadth].reshape(leading + (row_count, breadth))


def layer_norm(values, gain, shift):
    average = jnp.mean(values, axis=-1, keepdims=True)
    centred = values - average
    variance = jnp.mean(centred * centred, axis=-1, keepdims=True)
    inverse = lax.rsqrt(variance + EPSILON)
    normed = centred * inverse
    return (normed * gain + shift, normed, inverse)


def norm_backward(upstream, normed, inverse, gain):
    scaled_up = upstream * gain
    first_mean = jnp.mean(scaled_up, axis=-1, keepdims=True)
    second_mean = jnp.mean(scaled_up * normed, axis=-1, keepdims=True)
    grad_in = inverse * (scaled_up - first_mean - normed * second_mean)
    return (grad_in, jnp.sum(upstream * normed, axis=0), jnp.sum(upstream, axis=0))


def shards(
    hidden_in,
    query_weight,
    query_bias,
    key_weight,
    value_weight,
    value_bias,
    output_weight,
    output_bias,
    first_gain,
    first_shift,
    inner_weight,
    inner_bias,
    outer_weight,
    outer_bias,
    second_gain,
    second_shift,
    relative_table,
    segments,
    buckets,
    predicted,
    labels,
    cotangent,
):
    row_count, window, model_width = hidden_in.shape
    length = segments.shape[1]
    distances = 2 * length - 1
    span = window + length - 1
    pair_width = 2 * HEAD
    pair_count = model_width // pair_width
    score_scale = (3.0 * HEAD) ** (-0.5)
    window_start = lax.axis_index("seq") * window
    near_start = length - window - window_start
    token_count = row_count * window
    attention_set = (
        lax.all_gather(query_weight, ("fsdp", "seq"), axis=0, tiled=True),
        lax.all_gather(query_bias, ("fsdp", "seq"), axis=0, tiled=True),
        lax.all_gather(key_weight, ("fsdp", "seq"), axis=0, tiled=True),
        lax.all_gather(value_weight, ("fsdp", "seq"), axis=0, tiled=True),
        lax.all_gather(value_bias, ("fsdp", "seq"), axis=0, tiled=True),
        lax.all_gather(output_weight, ("fsdp", "seq"), axis=0, tiled=True),
        lax.all_gather(output_bias, ("fsdp", "seq"), axis=0, tiled=True),
        lax.all_gather(first_gain, ("fsdp", "seq"), axis=0, tiled=True),
        lax.all_gather(first_shift, ("fsdp", "seq"), axis=0, tiled=True),
        lax.all_gather(relative_table, ("fsdp", "seq"), axis=1, tiled=True),
    )
    feed_set = (
        lax.all_gather(inner_weight, ("fsdp", "seq"), axis=0, tiled=True),
        lax.all_gather(inner_bias, ("fsdp", "seq"), axis=0, tiled=True),
        lax.all_gather(outer_weight, ("fsdp", "seq"), axis=0, tiled=True),
        lax.all_gather(outer_bias, ("fsdp", "seq"), axis=0, tiled=True),
        lax.all_gather(second_gain, ("fsdp", "seq"), axis=0, tiled=True),
        lax.all_gather(second_shift, ("fsdp", "seq"), axis=0, tiled=True),
    )
    (
        query_matrix,
        query_offset,
        key_matrix,
        value_matrix,
        value_offset,
        output_matrix,
        output_offset,
        gain_first,
        shift_first,
        table_full,
    ) = attention_set
    inner_matrix, inner_offset, outer_matrix, outer_offset, gain_second, shift_second = feed_set
    tokens = hidden_in.reshape(token_count, model_width)
    queries = (
        (matmul("td,de->te", tokens, query_matrix) + query_offset.astype(jnp.float32))
        .astype(jnp.bfloat16)
        .reshape(row_count, window, model_width)
    )
    keys_own = (
        matmul("td,de->te", tokens, key_matrix)
        .astype(jnp.bfloat16)
        .reshape(row_count, window, model_width)
    )
    values_own = (
        (matmul("td,de->te", tokens, value_matrix) + value_offset.astype(jnp.float32))
        .astype(jnp.bfloat16)
        .reshape(row_count, window, model_width)
    )
    keys_all, values_all = (
        lax.all_gather(keys_own, "seq", axis=1, tiled=True),
        lax.all_gather(values_own, "seq", axis=1, tiled=True),
    )
    key_rel = matmul("pd,de->pe", table_full, key_matrix).astype(jnp.bfloat16)
    query_rel = (
        matmul("pd,de->pe", table_full, query_matrix) + query_offset.astype(jnp.float32)
    ).astype(jnp.bfloat16)
    reversed_buckets = buckets[::-1]
    table_rows = table_full.shape[0]
    one_hot = (
        reversed_buckets[:, None] == jnp.arange(table_rows, dtype=jnp.int32)[None, :]
    ).astype(jnp.bfloat16)
    bucket_keys = matmul("dp,pe->de", one_hot, key_rel).astype(jnp.bfloat16)
    bucket_queries = matmul("dp,pe->de", one_hot, query_rel).astype(jnp.bfloat16)
    near_keys = lax.dynamic_slice_in_dim(bucket_keys, near_start, span, 0)
    far_queries = lax.dynamic_slice_in_dim(bucket_queries, window_start, span, 0)
    segment_own = lax.dynamic_slice_in_dim(segments, window_start, window, 1)
    same_doc = (segment_own[:, :, None] == segments[:, None, :])[:, None]

    def pair_scores(pair_index):
        column = pair_index * pair_width
        query_pair = lax.dynamic_slice_in_dim(queries, column, pair_width, 2).reshape(
            row_count, window, 2, HEAD
        )
        key_pair = lax.dynamic_slice_in_dim(keys_all, column, pair_width, 2).reshape(
            row_count, length, 2, HEAD
        )
        value_pair = lax.dynamic_slice_in_dim(values_all, column, pair_width, 2).reshape(
            row_count, length, 2, HEAD
        )
        bucketkeys = lax.dynamic_slice_in_dim(near_keys, column, pair_width, 1).reshape(
            span, 2, HEAD
        )
        bucketqueries = lax.dynamic_slice_in_dim(far_queries, column, pair_width, 1).reshape(
            span, 2, HEAD
        )
        content = matmul("rihe,rjhe->rhij", query_pair, key_pair)
        near_scores = matmul("rihe,dhe->rhid", query_pair, bucketkeys)
        far_scores = matmul("rjhe,dhe->rhjd", key_pair, bucketqueries)
        to_position = skew_rows(near_scores, window - 1, length)
        from_position = jnp.swapaxes(skew_rows(far_scores, length - 1, window), 2, 3)
        summed = content + to_position + from_position
        masked = jnp.where(same_doc, summed * score_scale, NEGATIVE)
        return (masked, query_pair, key_pair, value_pair, bucketkeys, bucketqueries)

    def attend_pair(pair_index):
        masked, query_pair, key_pair, value_pair, bucketkeys, bucketqueries = pair_scores(
            pair_index
        )
        highest = jnp.max(masked, axis=-1, keepdims=True)
        expsum = jnp.exp(masked - highest)
        totals = jnp.sum(expsum, axis=-1, keepdims=True)
        weights_soft = (expsum / totals).astype(jnp.bfloat16)
        context_pair = matmul("rhij,rjhe->rihe", weights_soft, value_pair).astype(jnp.bfloat16)
        return (
            context_pair.reshape(row_count, window, pair_width),
            (highest + jnp.log(totals))[..., 0],
        )

    context_parts, log_totals = lax.map(attend_pair, jnp.arange(pair_count, dtype=jnp.int32))
    context = jnp.moveaxis(context_parts, 0, 2).reshape(token_count, model_width)
    attention_out = matmul("te,ed->td", context, output_matrix) + output_offset.astype(jnp.float32)
    residual_one = tokens.astype(jnp.float32) + attention_out
    first_out, first_normed, first_inverse = layer_norm(
        residual_one, gain_first.astype(jnp.float32), shift_first.astype(jnp.float32)
    )
    first_low = first_out.astype(jnp.bfloat16)
    inner_pre = matmul("td,df->tf", first_low, inner_matrix) + inner_offset.astype(jnp.float32)
    activated = jax.nn.gelu(inner_pre, approximate=False).astype(jnp.bfloat16)
    outer_out = matmul("tf,fd->td", activated, outer_matrix) + outer_offset.astype(jnp.float32)
    final_out, final_normed, final_inverse = layer_norm(
        first_out + outer_out, gain_second.astype(jnp.float32), shift_second.astype(jnp.float32)
    )
    result = final_out.astype(jnp.bfloat16).reshape(row_count, window, model_width)
    correct_count = lax.psum(jnp.sum((predicted == labels).astype(jnp.int32)), ("fsdp", "seq"))
    regathered = attention_set + feed_set
    (
        query_back,
        query_offset_back,
        key_back,
        value_back,
        value_offset_back,
        output_back,
        output_offset_back,
        gain_first_back,
        shift_first_back,
        table_back,
        inner_back,
        inner_offset_back,
        outer_back,
        outer_offset_back,
        gain_second_back,
        shift_second_back,
    ) = regathered
    upstream = cotangent.reshape(token_count, model_width).astype(jnp.float32)
    grad_sum2, grad_gain2, grad_shift2 = norm_backward(
        upstream, final_normed, final_inverse, gain_second_back.astype(jnp.float32)
    )
    grad_outer = grad_sum2.astype(jnp.bfloat16)
    outer_bias_part = jnp.sum(grad_outer.astype(jnp.float32), axis=0)
    outer_weight_part = matmul("tf,td->fd", activated, grad_outer)
    grad_act = matmul("td,fd->tf", grad_outer, outer_back).astype(jnp.bfloat16)
    _, gelu_back = jax.vjp(partial(jax.nn.gelu, approximate=False), inner_pre)
    grad_inner = gelu_back(grad_act.astype(jnp.float32))[0].astype(jnp.bfloat16)
    inner_bias_part = jnp.sum(grad_inner.astype(jnp.float32), axis=0)
    inner_weight_part = matmul("td,tf->df", first_low, grad_inner)
    grad_first = matmul("tf,df->td", grad_inner, inner_back) + grad_sum2
    feed_grads = (
        lax.psum_scatter(inner_weight_part, ("fsdp", "seq"), scatter_dimension=0, tiled=True),
        lax.psum_scatter(inner_bias_part, ("fsdp", "seq"), scatter_dimension=0, tiled=True),
        lax.psum_scatter(outer_weight_part, ("fsdp", "seq"), scatter_dimension=0, tiled=True),
        lax.psum_scatter(outer_bias_part, ("fsdp", "seq"), scatter_dimension=0, tiled=True),
        lax.psum_scatter(grad_gain2, ("fsdp", "seq"), scatter_dimension=0, tiled=True),
        lax.psum_scatter(grad_shift2, ("fsdp", "seq"), scatter_dimension=0, tiled=True),
    )
    grad_sum1, grad_gain1, grad_shift1 = norm_backward(
        grad_first, first_normed, first_inverse, gain_first_back.astype(jnp.float32)
    )
    grad_attention = grad_sum1.astype(jnp.bfloat16)
    output_bias_part = jnp.sum(grad_attention.astype(jnp.float32), axis=0)
    output_weight_part = matmul("te,td->ed", context, grad_attention)
    grad_context = (
        matmul("td,ed->te", grad_attention, output_back)
        .astype(jnp.bfloat16)
        .reshape(row_count, window, model_width)
    )

    def attend_back(pieces):
        pair_index, log_total = pieces
        masked, query_pair, key_pair, value_pair, bucketkeys, bucketqueries = pair_scores(
            pair_index
        )
        probability = jnp.exp(masked - log_total[..., None])
        grad_context_pair = lax.dynamic_slice_in_dim(
            grad_context, pair_index * pair_width, pair_width, 2
        ).reshape(row_count, window, 2, HEAD)
        grad_soft = matmul("rihe,rjhe->rhij", grad_context_pair, value_pair)
        grad_scores = probability * (
            grad_soft - jnp.sum(probability * grad_soft, axis=-1, keepdims=True)
        )
        grad_low = (grad_scores * score_scale).astype(jnp.bfloat16)
        grad_value = matmul("rhij,rihe->rjhe", probability.astype(jnp.bfloat16), grad_context_pair)
        grad_near = unskew_rows(grad_low, window - 1, span)
        grad_far = unskew_rows(jnp.swapaxes(grad_low, 2, 3), length - 1, span)
        grad_query = matmul("rhij,rjhe->rihe", grad_low, key_pair) + matmul(
            "rhid,dhe->rihe", grad_near, bucketkeys
        )
        grad_key = matmul("rhij,rihe->rjhe", grad_low, query_pair) + matmul(
            "rhjd,dhe->rjhe", grad_far, bucketqueries
        )
        grad_bkeys = matmul("rhid,rihe->dhe", grad_near, query_pair)
        grad_bqueries = matmul("rhjd,rjhe->dhe", grad_far, key_pair)
        return (
            grad_query.reshape(row_count, window, pair_width),
            grad_key.reshape(row_count, length, pair_width),
            grad_value.reshape(row_count, length, pair_width),
            grad_bkeys.reshape(span, pair_width),
            grad_bqueries.reshape(span, pair_width),
        )

    query_parts, key_parts, value_parts, bkey_parts, bquery_parts = lax.map(
        attend_back, (jnp.arange(pair_count, dtype=jnp.int32), log_totals)
    )
    grad_query_all = jnp.moveaxis(query_parts, 0, 2).reshape(token_count, model_width)
    grad_key_all = jnp.moveaxis(key_parts, 0, 2).reshape(row_count, length, model_width)
    grad_value_all = jnp.moveaxis(value_parts, 0, 2).reshape(row_count, length, model_width)
    near_grads = jnp.moveaxis(bkey_parts, 0, 1).reshape(span, model_width)
    far_grads = jnp.moveaxis(bquery_parts, 0, 1).reshape(span, model_width)
    grad_bucket_keys = lax.dynamic_update_slice_in_dim(
        jnp.zeros((distances, model_width), jnp.float32), near_grads, near_start, 0
    )
    grad_bucket_queries = lax.dynamic_update_slice_in_dim(
        jnp.zeros((distances, model_width), jnp.float32), far_grads, window_start, 0
    )
    key_grads, value_grads = (
        lax.psum_scatter(
            grad_key_all.astype(jnp.bfloat16), "seq", scatter_dimension=1, tiled=True
        ).astype(jnp.float32),
        lax.psum_scatter(
            grad_value_all.astype(jnp.bfloat16), "seq", scatter_dimension=1, tiled=True
        ).astype(jnp.float32),
    )
    query_low = grad_query_all.astype(jnp.bfloat16)
    key_low = key_grads.reshape(token_count, model_width).astype(jnp.bfloat16)
    value_low = value_grads.reshape(token_count, model_width).astype(jnp.bfloat16)
    grad_key_rel = jax.ops.segment_sum(grad_bucket_keys, reversed_buckets, num_segments=table_rows)
    grad_query_rel = jax.ops.segment_sum(
        grad_bucket_queries, reversed_buckets, num_segments=table_rows
    )
    query_token_part = matmul("td,te->de", tokens, query_low)
    query_bias_token = jnp.sum(query_low.astype(jnp.float32), axis=0)
    key_token_part = matmul("td,te->de", tokens, key_low)
    value_weight_part = matmul("td,te->de", tokens, value_low)
    value_bias_part = jnp.sum(value_low.astype(jnp.float32), axis=0)
    grad_input = (
        grad_sum1
        + matmul("te,de->td", query_low, query_back)
        + matmul("te,de->td", key_low, key_back)
        + matmul("te,de->td", value_low, value_back)
    )
    input_grad = grad_input.astype(jnp.bfloat16).reshape(row_count, window, model_width)
    key_rel_total, query_rel_total = lax.psum((grad_key_rel, grad_query_rel), ("fsdp", "seq"))
    attention_grads = (
        lax.psum_scatter(query_token_part, ("fsdp", "seq"), scatter_dimension=0, tiled=True),
        lax.psum_scatter(query_bias_token, ("fsdp", "seq"), scatter_dimension=0, tiled=True),
        lax.psum_scatter(key_token_part, ("fsdp", "seq"), scatter_dimension=0, tiled=True),
        lax.psum_scatter(value_weight_part, ("fsdp", "seq"), scatter_dimension=0, tiled=True),
        lax.psum_scatter(value_bias_part, ("fsdp", "seq"), scatter_dimension=0, tiled=True),
        lax.psum_scatter(output_weight_part, ("fsdp", "seq"), scatter_dimension=0, tiled=True),
        lax.psum_scatter(output_bias_part, ("fsdp", "seq"), scatter_dimension=0, tiled=True),
        lax.psum_scatter(grad_gain1, ("fsdp", "seq"), scatter_dimension=0, tiled=True),
        lax.psum_scatter(grad_shift1, ("fsdp", "seq"), scatter_dimension=0, tiled=True),
    )
    shard_rows = query_weight.shape[0]
    shard_start = lax.axis_index(("fsdp", "seq")) * shard_rows
    table_shard = relative_table.astype(jnp.float32)
    query_weight_grad = attention_grads[0] + precise("pd,pe->de", table_shard, query_rel_total)
    key_weight_grad = attention_grads[2] + precise("pd,pe->de", table_shard, key_rel_total)
    query_bias_grad = attention_grads[1] + jnp.sum(
        lax.dynamic_slice_in_dim(query_rel_total, shard_start, shard_rows, 1), axis=0
    )
    relative_table_grad = precise(
        "pe,de->pd", query_rel_total, query_weight.astype(jnp.float32)
    ) + precise("pe,de->pd", key_rel_total, key_weight.astype(jnp.float32))
    return (
        result,
        input_grad,
        query_weight_grad,
        query_bias_grad,
        key_weight_grad,
        attention_grads[3],
        attention_grads[4],
        attention_grads[5],
        attention_grads[6],
        attention_grads[7],
        attention_grads[8],
        feed_grads[0],
        feed_grads[1],
        feed_grads[2],
        feed_grads[3],
        feed_grads[4],
        feed_grads[5],
        relative_table_grad,
        correct_count,
    )


def solution(mesh):
    return jax.shard_map(
        shards,
        mesh=mesh,
        in_specs=(
            P("fsdp", "seq", None),
            P(("fsdp", "seq"), None),
            P(("fsdp", "seq")),
            P(("fsdp", "seq"), None),
            P(("fsdp", "seq"), None),
            P(("fsdp", "seq")),
            P(("fsdp", "seq"), None),
            P(("fsdp", "seq")),
            P(("fsdp", "seq")),
            P(("fsdp", "seq")),
            P(("fsdp", "seq"), None),
            P(("fsdp", "seq")),
            P(("fsdp", "seq"), None),
            P(("fsdp", "seq")),
            P(("fsdp", "seq")),
            P(("fsdp", "seq")),
            P(None, ("fsdp", "seq")),
            P("fsdp", None),
            P(),
            P("fsdp", "seq"),
            P("fsdp", "seq"),
            P("fsdp", "seq", None),
        ),
        out_specs=(
            P("fsdp", "seq", None),
            P("fsdp", "seq", None),
            P(("fsdp", "seq"), None),
            P(("fsdp", "seq")),
            P(("fsdp", "seq"), None),
            P(("fsdp", "seq"), None),
            P(("fsdp", "seq")),
            P(("fsdp", "seq"), None),
            P(("fsdp", "seq")),
            P(("fsdp", "seq")),
            P(("fsdp", "seq")),
            P(("fsdp", "seq"), None),
            P(("fsdp", "seq")),
            P(("fsdp", "seq"), None),
            P(("fsdp", "seq")),
            P(("fsdp", "seq")),
            P(("fsdp", "seq")),
            P(None, ("fsdp", "seq")),
            P(),
        ),
        check_vma=False,
    )
```

profile of v0, /device:TPU:0, one launch (start us, length us, event | category | flops | bytes accessed | tf_op | source)
XLA Modules:
  0.0 1851.7 jit_solution(3494316236153057164)
XLA Ops:
  18.9 42.5 %all-reduce.24 = (bf16[3072]{0:T(1024)(128)(2,1)S(1)}, bf16[768]{0:T(1024)(128)(2,1)S(1)}, bf16[768]{0:T(1024)(128)(2,1)S(1)}, bf16[768]{0:T(1024)(128)(2,1)S(1)...) all-reduce(bf16[3072]{0:T(1024)(128)(2,1)S(1)} %dynamic-update-slic, ...), channel_id=1, replica_groups=mesh['fsdp'=16,'seq'=2] {'fsdp','seq'}, use_global_device_ids=true, to_apply=%add.9 | all-reduce | flops 9216 | bytes 36864
  63.1 42.9 %all_gather.61 = bf16[512,768]{0,1:T(8,128)(2,1)S(1)} all-gather(bf16[512,24]{0,1:T(8,128)(2,1)} %param.42), channel_id=1, replica_groups=mesh['fsdp'=16,'seq'=2] {'fsdp','seq'}, dimensions={1}, use_global_device_ids=true | all-gather | bytes 811008 | tf_op jit(solution)/shard_map/all_gather | solution.py:109
  114.1 9.8 all-gather.11.cloned.1.call-done
  126.6 53.0 %all-gather.13.cloned.1.call-done = bf16[768,768]{1,0:T(8,128)(2,1)} async-done(((bf16[24,768]{1,0:T(8,128)(2,1)}), bf16[768,768]{1,0:T(8,128)(2,1)}) %all-gather.13.cloned.1.call-update) | async-done | bytes 1179664 | tf_op jit(solution)/shard_map/all_gather | solution.py:102
  197.6 240.7 %while.32 = (s32[]{:T(128)}, bf16[6,1,256,128]{2,3,1,0:T(8,128)(2,1)}, f32[6,1,2,256]{3,2,1,0:T(2,128)}, s32[6]{0:T(128)S(1)}, bf16[1,512,768]{1,2,0:T(8,128)(2,...) while((s32[]{:T(128)}, ...), condition=%wide.region_3.4_spmd.clone, body=%wide.region_0.3_spmd.clone.sunk | while | flops 220691968 | bytes 55185396 | solution.py:208
  204.7 6.2 reshape.522
  210.9 4.5 dynamic_slice.137
  215.4 6.7 reshape.523
  244.8 6.2 reshape.522
  251.0 4.5 dynamic_slice.137
  255.5 6.7 reshape.523
  284.9 6.2 reshape.522
  291.1 4.5 dynamic_slice.137
  295.5 6.7 reshape.523
  324.9 6.2 reshape.522
  331.1 4.5 dynamic_slice.137
  335.6 6.7 reshape.523
  364.9 6.2 reshape.522
  371.1 4.5 dynamic_slice.137
  375.6 6.7 reshape.523
  404.9 6.2 reshape.522
  411.1 4.5 dynamic_slice.137
  415.6 6.7 reshape.523
  440.7 11.4 multiply_convert_fusion
  466.9 499.4 %while.33 = (s32[]{:T(128)}, bf16[6,1,256,128]{2,3,1,0:T(8,128)(2,1)}, bf16[6,1,512,128]{2,3,1,0:T(8,128)(2,1)}, bf16[6,1,512,128]{2,3,1,0:T(8,128)(2,1)}, f32[6...) while((s32[]{:T(128)}, ...), condition=%wide.region_14.15_spmd.clone, body=%wide.region_12.14_spmd.clone.sunk | while | flops 623640064 | bytes 105583208 | solution.py:309
  497.8 6.2 reshape.526
  504.0 4.5 dynamic_slice.147
  508.4 6.7 reshape.527
  557.6 5.1 reshape.535
  576.0 6.2 reshape.526
  582.2 4.5 dynamic_slice.147
  586.7 6.7 reshape.527
  635.9 5.1 reshape.535
  654.3 6.2 reshape.526
  660.5 4.5 dynamic_slice.147
  665.0 6.7 reshape.527
  714.2 5.1 reshape.535
  732.6 6.2 reshape.526
  738.7 4.5 dynamic_slice.147
  743.2 6.7 reshape.527
  792.4 5.1 reshape.535
  810.8 6.2 reshape.526
  817.0 4.5 dynamic_slice.147
  821.5 6.7 reshape.527
  870.6 5.1 reshape.535
  889.1 6.2 reshape.526
  895.2 4.5 dynamic_slice.147
  899.7 6.7 reshape.527
  948.9 5.1 reshape.535
  974.3 6.9 dynamic_update_slice.38
  981.1 9.2 scatter_custom_fusion
  992.1 6.4 dynamic_update_slice.39
  998.5 9.2 scatter_custom_fusion.1
  1023.5 5.2 fusion.87
  1030.4 5.1 fusion.84
  1036.8 39.0 %psum.23 = s32[]{:T(128)} all-reduce(s32[]{:T(128)} %fusion.80), channel_id=1, replica_groups=mesh['fsdp'=16,'seq'=2] {'fsdp','seq'}, use_global_device_ids=true, to_apply=%region_47.48 | all-reduce | flops 1 | bytes 8 | tf_op jit(solution)/shard_map/psum | solution.py:223
  1077.8 41.8 %all-reduce.22 = (f32[768]{0:T(1024)S(1)}, f32[768]{0:T(1024)S(1)}, f32[768]{0:T(1024)S(1)}, f32[768]{0:T(1024)S(1)}, f32[768]{0:T(1024)S(1)}, /*index=5*/f32[30...) all-reduce(f32[768]{0:T(1024)S(1)} %bitcast.460, ...), channel_id=7, replica_groups=mesh['fsdp'=16,'seq'=2] {'fsdp','seq'}, use_global_device_ids=true, to_apply=%region_21.22.clone | all-reduce | flops 9216 | bytes 73728
  1124.2 21.0 %all-reduce.27.cloned.1.call-done = (f32[512,768]{1,0:T(8,128)}, f32[512,768]{1,0:T(8,128)}) async-done(((f32[512,768]{1,0:T(8,128)}, f32[512,768]{1,0:T(8,128)}), (f32[512,768]{1,0:T(8,128)}, f32[512,768]{1,0:T(8,128)})) %all-reduce.27.cloned.1.call-update) | async-done | bytes 3145744 | tf_op jit(solution)/shard_map/psum | solution.py:350
  1155.0 94.1 %reduce-scatter.25.cloned.1.call-done = f32[24,768]{1,0:T(8,128)} async-done(((f32[768,768]{1,0:T(8,128)}), f32[24,768]{1,0:T(8,128)}) %reduce-scatter.25.cloned.1.call-update) | async-done | bytes 73744 | tf_op jit(solution)/shard_map/reduce_scatter | solution.py:352
  1251.2 101.8 %reduce-scatter.27.cloned.1.call-done = f32[24,768]{1,0:T(8,128)} async-done(((f32[768,768]{1,0:T(8,128)}), f32[24,768]{1,0:T(8,128)}) %reduce-scatter.27.cloned.1.call-update) | async-done | bytes 73744 | tf_op jit(solution)/shard_map/reduce_scatter | solution.py:354
  1355.1 102.3 %reduce-scatter.19.cloned.1.call-done = f32[24,768]{1,0:T(8,128)} async-done(((f32[768,768]{1,0:T(8,128)}), f32[24,768]{1,0:T(8,128)}) %reduce-scatter.19.cloned.1.call-update) | async-done | bytes 73744 | tf_op jit(solution)/shard_map/reduce_scatter | solution.py:357
  1457.3 104.5 %reduce-scatter.29.cloned.1.call-done = f32[24,768]{1,0:T(8,128)} async-done(((f32[768,768]{1,0:T(8,128)}), f32[24,768]{1,0:T(8,128)}) %reduce-scatter.29.cloned.1.call-update) | async-done | bytes 73744
  1561.8 141.6 %reduce-scatter.21.cloned.1.call-done = f32[24,3072]{1,0:T(8,128)} async-done(((f32[768,3072]{1,0:T(8,128)}), f32[24,3072]{1,0:T(8,128)}) %reduce-scatter.21.cloned.1.call-update) | async-done | bytes 294928 | tf_op jit(solution)/shard_map/reduce_scatter | solution.py:257
  1703.5 141.5 %reduce-scatter.23.cloned.1.call-done = f32[96,768]{1,0:T(8,128)} async-done(((f32[3072,768]{1,0:T(8,128)}), f32[96,768]{1,0:T(8,128)}) %reduce-scatter.23.cloned.1.call-update) | async-done | bytes 294928 | tf_op jit(solution)/shard_map/reduce_scatter | solution.py:259
  (780 shorter events, 568.6 us)
Async XLA Ops:
  7.2 101.5 %all-gather.9.cloned.1.call-start = ((), (), s32[]{:S(2)}) async-start(), calls=%async_computation.8 | async-start | bytes 1216512 | tf_op jit(solution)/shard_map/all_gather | solution.py:103
  7.9 116.0 %all-gather.11.cloned.1.call-start = ((), (), s32[]{:S(2)}) async-start(), calls=%async_computation.9 | async-start | bytes 1216512 | tf_op jit(solution)/shard_map/all_gather | solution.py:100
  8.7 171.0 %all-gather.13.cloned.1.call-start = ((), (), s32[]{:S(2)}) async-start(), calls=%async_computation.10 | async-start | bytes 1216512 | tf_op jit(solution)/shard_map/all_gather | solution.py:102
  9.4 428.9 %all-gather.15.cloned.1.call-start = ((), (), s32[]{:S(2)}) async-start(), calls=%async_computation.11 | async-start | bytes 1216512 | tf_op jit(solution)/shard_map/all_gather | solution.py:105
  10.0 113.9 %copy-start.13 = (bf16[1,256,768]{2,1,0:T(8,128)(2,1)S(1)}, bf16[1,256,768]{2,1,0:T(8,128)(2,1)}, u32[]{:S(2)}) copy-start(bf16[1,256,768]{2,1,0:T(8,128)(2,1)} %param.26) | copy-start | bytes 1179652
  10.0 430.7 %all-gather.17.cloned.1.call-start = ((), (), s32[]{:S(2)}) async-start(), calls=%async_computation.12 | async-start | bytes 4866048 | tf_op jit(solution)/shard_map/all_gather | solution.py:112
  10.6 441.5 %all-gather.19.cloned.1.call-start = ((), (), s32[]{:S(2)}) async-start(), calls=%async_computation.13 | async-start | bytes 4866048 | tf_op jit(solution)/shard_map/all_gather | solution.py:114
  11.2 999.2 %reduce-scatter.15.cloned.1.call-start = ((), (), s32[]{:S(2)}) async-start(), calls=%async_computation.14 | async-start | bytes 1179648 | tf_op jit(solution)/shard_map/reduce_scatter | solution.py:324
  106.8 84.6 %copy-start.54 = (s32[1023]{0:T(1024)}, s32[1023]{0:T(1024)S(1)}, u32[]{:S(2)}) copy-start(s32[1023]{0:T(1024)S(1)} %slice.32) | copy-start | bytes 12280
  106.8 345.3 %copy-start.40 = (f32[768]{0:T(1024)}, f32[768]{0:T(1024)S(1)}, u32[]{:S(2)}) copy-start(f32[768]{0:T(1024)S(1)} %convert_element_type.201) | copy-start | bytes 9220
  106.8 357.7 %copy-start.37 = (f32[768]{0:T(1024)}, f32[768]{0:T(1024)S(1)}, u32[]{:S(2)}) copy-start(f32[768]{0:T(1024)S(1)} %convert_element_type.200) | copy-start | bytes 9220
  440.4 24.2 %copy-start.11 = (f32[256,768]{1,0:T(8,128)}, f32[256,768]{1,0:T(8,128)S(1)}, u32[]{:S(2)}) copy-start(f32[256,768]{1,0:T(8,128)S(1)} %get-tuple-element.461) | copy-start | bytes 2359300
  440.4 24.2 %copy-start.43 = (f32[256]{0:T(256)}, f32[256]{0:T(256)S(1)}, u32[]{:S(2)}) copy-start(f32[256]{0:T(256)S(1)} %broadcast_multiply_fusion.5) | copy-start | bytes 3076
  440.6 23.9 %copy-start.49 = (f32[256]{0:T(256)}, f32[256]{0:T(256)S(1)}, u32[]{:S(2)}) copy-start(f32[256]{0:T(256)S(1)} %add_rsqrt_fusion.1) | copy-start | bytes 3076
  440.7 11.4 copy-start.53
  452.1 7.5 slice-start.2
  452.1 7.4 slice-start.3
  452.1 7.4 copy-start.62
  520.7 11.0 copy-start.5
  535.0 6.8 copy-start.2
  535.1 8.6 copy-start.8
  555.5 7.3 copy-start.4
  598.9 11.0 copy-start.5
  613.3 6.8 copy-start.2
  613.3 8.6 copy-start.8
  633.7 7.3 copy-start.4
  677.2 11.0 copy-start.5
  691.6 6.8 copy-start.2
  691.6 8.6 copy-start.8
  712.0 7.3 copy-start.4
  755.4 11.0 copy-start.5
  769.8 6.8 copy-start.2
  769.9 8.6 copy-start.8
  790.2 7.3 copy-start.4
  833.7 11.0 copy-start.5
  848.1 6.8 copy-start.2
  848.1 8.6 copy-start.8
  868.5 7.3 copy-start.4
  911.9 11.0 copy-start.5
  926.3 6.8 copy-start.2
  926.3 8.6 copy-start.8
  946.7 7.3 copy-start.4
  966.3 50.7 %reduce-scatter.17.cloned.1.call-start = ((), (), s32[]{:S(2)}) async-start(), calls=%async_computation.15 | async-start | bytes 1179648 | tf_op jit(solution)/shard_map/reduce_scatter | solution.py:327
  967.0 178.2 %all-reduce.27.cloned.1.call-start = ((), (), s32[]{:S(2)}) async-start(), calls=%async_computation.22 | async-start | bytes 6291456 | tf_op jit(solution)/shard_map/psum | solution.py:350
  998.5 9.3 copy-start.14
  998.5 9.3 copy-start.19
  1007.7 241.3 %reduce-scatter.25.cloned.1.call-start = ((), (), s32[]{:S(2)}) async-start(), calls=%async_computation.19 | async-start | bytes 2433024 | tf_op jit(solution)/shard_map/reduce_scatter | solution.py:352
  1010.3 342.7 %reduce-scatter.27.cloned.1.call-start = ((), (), s32[]{:S(2)}) async-start(), calls=%async_computation.20 | async-start | bytes 2433024 | tf_op jit(solution)/shard_map/reduce_scatter | solution.py:354
  1013.8 443.5 %reduce-scatter.19.cloned.1.call-start = ((), (), s32[]{:S(2)}) async-start(), calls=%async_computation.16 | async-start | bytes 2433024 | tf_op jit(solution)/shard_map/reduce_scatter | solution.py:357
  1016.9 544.9 %reduce-scatter.29.cloned.1.call-start = ((), (), s32[]{:S(2)}) async-start(), calls=%async_computation.21 | async-start | bytes 2433024
  1023.1 680.3 %reduce-scatter.21.cloned.1.call-start = ((), (), s32[]{:S(2)}) async-start(), calls=%async_computation.17 | async-start | bytes 9732096 | tf_op jit(solution)/shard_map/reduce_scatter | solution.py:257
  1028.7 816.2 %reduce-scatter.23.cloned.1.call-start = ((), (), s32[]{:S(2)}) async-start(), calls=%async_computation.18 | async-start | bytes 9732096 | tf_op jit(solution)/shard_map/reduce_scatter | solution.py:259
  1035.4 40.4 %copy-start.22 = (bf16[1,256,768]{2,1,0:T(8,128)(2,1)S(1)}, bf16[1,256,768]{2,1,0:T(8,128)(2,1)}, u32[]{:S(2)}) copy-start(bf16[1,256,768]{2,1,0:T(8,128)(2,1)} %param.47) | copy-start | bytes 1179652
  1035.4 40.5 %copy-start.20 = (bf16[6,1,256,128]{2,3,1,0:T(8,128)(2,1)S(1)}, bf16[6,1,256,128]{2,3,1,0:T(8,128)(2,1)}, u32[]{:S(2)}) copy-start(bf16[6,1,256,128]{2,3,1,0:T(8,128)(2,1)} %get-tuple-element.155) | copy-start | bytes 1179652
  1035.4 40.6 %copy-start.34 = (bf16[768,768]{1,0:T(8,128)(2,1)S(1)}, bf16[768,768]{1,0:T(8,128)(2,1)}, u32[]{:S(2)}) copy-start(bf16[768,768]{1,0:T(8,128)(2,1)} %all-gather.11.cloned.1.call-done) | copy-start | bytes 3538948
  1036.1 41.4 %copy-start.23 = (bf16[1,256,768]{1,2,0:T(8,128)(2,1)S(1)}, bf16[1,256,768]{1,2,0:T(8,128)(2,1)}, u32[]{:S(2)}) copy-start(bf16[1,256,768]{1,2,0:T(8,128)(2,1)} %reduce-scatter.17.cloned.1.call-done) | copy-start | bytes 1179652
  1036.1 41.6 %copy-start.46 = (f32[768]{0:T(1024)S(1)}, f32[768]{0:T(1024)}, u32[]{:S(2)}) copy-start(f32[768]{0:T(1024)} %get-tuple-element.362) | copy-start | bytes 9220
  1036.1 41.6 %copy-start.47 = (f32[768]{0:T(1024)S(1)}, f32[768]{0:T(1024)}, u32[]{:S(2)}) copy-start(f32[768]{0:T(1024)} %get-tuple-element.441) | copy-start | bytes 9220
  1036.1 41.6 %copy-start.48 = (f32[768]{0:T(1024)S(1)}, f32[768]{0:T(1024)}, u32[]{:S(2)}) copy-start(f32[768]{0:T(1024)} %get-tuple-element.443) | copy-start | bytes 9220
  1036.1 41.6 %copy-start.52 = (f32[3072]{0:T(1024)S(1)}, f32[3072]{0:T(1024)}, u32[]{:S(2)}) copy-start(f32[3072]{0:T(1024)} %get-tuple-element.466) | copy-start | bytes 36868
  1036.2 41.6 %copy-start.55 = (f32[768]{0:T(1024)S(1)}, f32[768]{0:T(1024)}, u32[]{:S(2)}) copy-start(f32[768]{0:T(1024)} %get-tuple-element.360) | copy-start | bytes 9220
  1036.2 41.6 %copy-start.56 = (f32[768]{0:T(1024)S(1)}, f32[768]{0:T(1024)}, u32[]{:S(2)}) copy-start(f32[768]{0:T(1024)} %get-tuple-element.365) | copy-start | bytes 9220
  1145.2 6.7 copy-start.15
  1151.9 97.2 %copy-start.36 = (bf16[512,24]{0,1:T(8,128)(2,1)S(1)}, bf16[512,24]{0,1:T(8,128)(2,1)}, u32[]{:S(2)}) copy-start(bf16[512,24]{0,1:T(8,128)(2,1)} %param.42) | copy-start | bytes 73732
  (88 other events, 298.5 us)
Sparse Core Ops, SparseCore 0:
  10.9 56.9 all-gather.8
  70.7 53.0 all-gather.10
  126.8 52.8 all-gather.12
  182.4 52.8 all-gather.14
  238.0 62.5 all-gather.16
  303.3 61.8 all-gather.18
  966.4 7.1 reduce-scatter.14
  975.8 9.2 reduce-scatter.16
  1007.9 137.3 all-reduce.26
  1150.4 98.6 reduce-scatter.24
  1254.4 98.5 reduce-scatter.26
  1358.7 98.6 reduce-scatter.18
  1463.2 98.5 reduce-scatter.28
  1568.2 135.2 reduce-scatter.20
  1709.8 135.1 reduce-scatter.22
where the time goes:
time: 1870 us; the launch traced here: 1850 us
  waiting for transfers between devices  774 us (41%)
  local copies, waits for them, and re-layouts  674 us (36%)
  blocking collectives  171 us (9%)
  matrix products  141 us (8%)
  loops' own time  40.3 us (2%)
  other arithmetic  36.6 us (2%)
    reduce_scatter x1, waiting for transfers between devices, shards(): lax.psum_scatter(inner_weight_part, ('fsdp', 'seq'), scatter_dimension=0,...  142 us
    reduce_scatter x1, waiting for transfers between devices, shards(): lax.psum_scatter(outer_weight_part, ('fsdp', 'seq'), scatter_dimension=0,...  141 us
    dot_general x110, matrix products, matmul(): return jnp.einsum(spec, left, right, preferred_element_type=jnp.float32)  133 us
    reshape x24, local copies, waits for them, and re-layouts, skew_rows(): return selected.reshape(leading + (row_count, breadth - 1))[..., :columns]  116 us
    unnamed x16, waiting for transfers between devices  109 us
    reshape x24, local copies, waits for them, and re-layouts, skew_rows(): flattened = scores_in.reshape(leading + (row_count * breadth,))  108 us
    reduce_scatter x1, waiting for transfers between devices, shards(): lax.psum_scatter(output_weight_part, ('fsdp', 'seq'), scatter_dimension=0...  102 us
    reduce_scatter x1, waiting for transfers between devices, shards(): lax.psum_scatter(key_token_part, ('fsdp', 'seq'), scatter_dimension=0, ti...  102 us
  transfers between devices with their start and end apart: 15, of which 9 were waited for; matrix products, arithmetic and copies ran while one was open for 20% of the time, Pallas kernels for 0%

commit v1 on v0

--- a/solution.py
+++ b/solution.py
@@ -2,7 +2,10 @@
 
 import jax
 import jax.numpy as jnp
+import numpy as np
 from jax import lax
+from jax.experimental import pallas as pl
+from jax.experimental.pallas import tpu as pltpu
 from jax.sharding import PartitionSpec as P
 
 HEAD = 64
@@ -393,9 +396,1025 @@
     )
 
 
+MESH = pl.DeviceIdType.MESH
+F32 = jnp.float32
+BF16 = jnp.bfloat16
+
+
+def dot(left, right, left_dim=1, right_dim=0):
+    return lax.dot_general(
+        left, right, (((left_dim,), (right_dim,)), ((), ())), preferred_element_type=F32
+    )
+
+
+def low(value):
+    return value.astype(BF16)
+
+
+class Route:
+    def __init__(self):
+        chip = lax.axis_index("fsdp")
+        self.core = lax.axis_index("seq")
+        self.other = 1 - self.core
+        self.chip = chip
+        self.x = chip % 2
+        self.y = (chip // 2) % 2
+        self.z = chip // 4
+        self.plane = chip % 4
+        self.plane_x = self.plane + 1 - 2 * self.x
+        self.plane_y = self.plane + 2 - 4 * self.y
+        self.partner = (chip, self.other)
+        self.at_x = (self.z * 4 + self.plane_x, self.core)
+        self.at_y = (self.z * 4 + self.plane_y, self.core)
+
+    def at_line(self, line):
+        return (line * 4 + self.plane, self.core)
+
+    def ahead(self, step):
+        return (self.z + step) % LINE
+
+    def behind(self, step):
+        return (self.z + LINE - step) % LINE
+
+
+def remote(source, target, send_sem, recv_sem, device):
+    return pltpu.make_async_remote_copy(
+        source, target, send_sem, recv_sem, device_id=device, device_id_type=MESH
+    )
+
+
+class Gather:
+    def __init__(self, route, arrays, send, recv):
+        self.r, self.arrays, self.send, self.recv = route, arrays, send, recv
+
+    def copy(self, which, kind, send_at, recv_at, line, plane, device):
+        block = self.arrays[which].at[line, plane]
+        return remote(
+            block,
+            block,
+            self.send.at[which, kind, send_at],
+            self.recv.at[which, kind, recv_at],
+            device,
+        )
+
+    def along_line(self, step):
+        r = self.r
+        return [
+            self.copy(i, 0, step, r.z, r.z, r.plane, r.at_line(r.ahead(step)))
+            for i in range(len(self.arrays))
+        ]
+
+    def to_sides(self, line):
+        r = self.r
+        return [
+            self.copy(i, kind, line, line, line, r.plane, device)
+            for i in range(len(self.arrays))
+            for kind, device in ((1, r.at_x), (2, r.at_y))
+        ]
+
+    def to_corner(self, line):
+        r = self.r
+        return [
+            self.copy(
+                i,
+                3,
+                line,
+                line,
+                line,
+                r.plane_y if i == 1 else r.plane_x,
+                r.at_x if i == 1 else r.at_y,
+            )
+            for i in range(len(self.arrays))
+        ]
+
+    def start(self):
+        for step in range(1, LINE):
+            for copy in self.along_line(step):
+                copy.start()
+        for copy in self.to_sides(self.r.z):
+            copy.start()
+
+    def got_line(self, step):
+        r = self.r
+        line = r.behind(step)
+        for i in range(len(self.arrays)):
+            self.copy(i, 0, step, line, line, r.plane, r.at_line(line)).wait_recv()
+
+    def got_sides(self, line):
+        r = self.r
+        for i in range(len(self.arrays)):
+            self.copy(i, 1, line, line, line, r.plane_x, r.at_x).wait_recv()
+            self.copy(i, 2, line, line, line, r.plane_y, r.at_y).wait_recv()
+
+    def got_corner(self, line):
+        r = self.r
+        for i in range(len(self.arrays)):
+            self.copy(i, 3, line, line, line, 3 - r.plane, r.at_y).wait_recv()
+
+    def turn(self, step):
+        self.got_line(step)
+        for copy in self.to_sides(self.r.behind(step)):
+            copy.start()
+        self.corner(step - 1)
+
+    def corner(self, step):
+        line = self.r.behind(step) if step else self.r.z
+        self.got_sides(line)
+        for copy in self.to_corner(line):
+            copy.start()
+
+    def finish(self):
+        for line in range(LINE):
+            self.got_corner(line)
+
+    def sent(self):
+        for step in range(1, LINE):
+            for copy in self.along_line(step):
+                copy.wait_send()
+        for line in range(LINE):
+            for copy in self.to_sides(line) + self.to_corner(line):
+                copy.wait_send()
+
+
+class Scatter:
+    def __init__(self, route, arrays, first, second, last, send, recv):
+        self.r, self.arrays = route, arrays
+        self.first, self.second, self.last = first, second, last
+        self.send, self.recv = send, recv
+
+    def side(self, i, k):
+        r = self.r
+        return (1 - r.x) + 2 * k if i == 0 else 2 * (1 - r.y) + k
+
+    def kept(self, i, k):
+        r = self.r
+        return r.x + 2 * k if i == 0 else 2 * r.y + k
+
+    def step_one(self, line, which=(0, 1)):
+        r = self.r
+        return [
+            remote(
+                self.arrays[i].at[line, self.side(i, k)],
+                self.first[i].at[line, k],
+                self.send.at[i, k, line],
+                self.recv.at[i, k, line],
+                r.at_x if i == 0 else r.at_y,
+            )
+            for i in which
+            for k in (0, 1)
+        ]
+
+    def step_two(self, line):
+        r = self.r
+        return [
+            remote(
+                self.arrays[i].at[line, r.plane_y if i == 0 else r.plane_x],
+                self.second[i].at[line],
+                self.send.at[i, 2, line],
+                self.recv.at[i, 2, line],
+                r.at_y if i == 0 else r.at_x,
+            )
+            for i in (0, 1)
+        ]
+
+    def step_line(self, step):
+        r = self.r
+        line = r.ahead(step)
+        return [
+            remote(
+                self.arrays[i].at[line, r.plane],
+                self.last[i].at[r.z],
+                self.send.at[i, 3, step],
+                self.recv.at[i, 3, r.z],
+                r.at_line(line),
+            )
+            for i in (0, 1)
+        ]
+
+    def one(self, step, which=(0, 1)):
+        for copy in self.step_one(self.r.ahead(step), which):
+            copy.start()
+
+    def two(self, step):
+        line = self.r.ahead(step)
+        for copy in self.step_one(line):
+            copy.wait_recv()
+        for i in (0, 1):
+            for k in (0, 1):
+                at = self.arrays[i].at[line, self.kept(i, k)]
+                at[...] = low(at[...].astype(F32) + self.first[i][line, k].astype(F32))
+        for copy in self.step_two(line):
+            copy.start()
+
+    def three(self, step, last=False):
+        line = self.r.ahead(step)
+        for copy in self.step_two(line):
+            copy.wait_recv()
+        for i in (0, 1):
+            at = self.arrays[i].at[line, self.r.plane]
+            at[...] = low(at[...].astype(F32) + self.second[i][line].astype(F32))
+        if not last:
+            for copy in self.step_line(step):
+                copy.start()
+
+    def total(self, i):
+        r = self.r
+        value = self.arrays[i][r.z, r.plane].astype(F32)
+        for step in range(1, LINE):
+            value = value + self.last[i][r.behind(step)].astype(F32)
+        return value
+
+    def finish(self):
+        r = self.r
+        for step in range(1, LINE):
+            line = r.behind(step)
+            for i in (0, 1):
+                remote(
+                    self.arrays[i].at[line, r.plane],
+                    self.last[i].at[line],
+                    self.send.at[i, 3, step],
+                    self.recv.at[i, 3, line],
+                    r.at_line(line),
+                ).wait_recv()
+
+    def sent(self):
+        for line in range(LINE):
+            for copy in self.step_one(line) + self.step_two(line):
+                copy.wait_send()
+        for step in range(1, LINE):
+            for copy in self.step_line(step):
+                copy.wait_send()
+
+
+def loop(count, body):
+    def step(index, carry):
+        body(index)
+        return carry
+
+    lax.fori_loop(0, count, step, 0)
+
+
+def aligned(index, size):
+    return pl.ds(pl.multiple_of(index * size, size), size)
+
+
+def erf_parts(value):
+    tail = lax.erf(value * np.float32(0.5**0.5))
+    half = 0.5 * (1.0 + tail)
+    density = jnp.exp(value * value * -0.5) * np.float32((2.0 * np.pi) ** -0.5)
+    return value * half, half + value * density
+
+
+def norm(values, gain, shift):
+    average = jnp.mean(values, axis=-1, keepdims=True)
+    centred = values - average
+    variance = jnp.mean(centred * centred, axis=-1, keepdims=True)
+    inverse = lax.rsqrt(variance + EPSILON)
+    normed = centred * inverse
+    return normed * gain + shift, normed, inverse
+
+
+def norm_pull(upstream, normed, inverse, gain):
+    scaled_up = upstream * gain
+    first_mean = jnp.mean(scaled_up, axis=-1, keepdims=True)
+    second_mean = jnp.mean(scaled_up * normed, axis=-1, keepdims=True)
+    return inverse * (scaled_up - first_mean - normed * second_mean)
+
+
+def layer_kernel(names, *refs):
+    b = dict(zip(names, refs))
+    at = type("Refs", (), b)
+    r = Route()
+    core, other = r.core, r.other
+    own_rows = aligned(core, 256)
+    other_rows = aligned(other, 256)
+    score_scale = np.float32((3.0 * HEAD) ** (-0.5))
+
+    barrier = pltpu.get_barrier_semaphore()
+    friends = [r.partner, r.at_x, r.at_y] + [r.at_line(r.ahead(k)) for k in range(1, LINE)]
+    for device in friends:
+        pl.semaphore_signal(barrier, inc=1, device_id=device, device_id_type=MESH)
+
+    waiting = []
+
+    def swap(slot, source, target):
+        copy = remote(source, target, at.swap_send.at[slot], at.swap_recv.at[slot], r.partner)
+        copy.start()
+        waiting.append(copy)
+        return copy
+
+    gather_one = Gather(r, (at.gat_a, at.gat_b, at.gat_s), at.ga_send, at.ga_recv)
+    gather_two = Gather(r, (at.gat_1, at.gat_2), at.gf_send, at.gf_recv)
+
+    at.sums[...] = jnp.zeros_like(at.sums)
+    right = (at.predicted[...] == at.labels[...]).astype(F32)
+    at.sums[10:11, :] = jnp.broadcast_to(jnp.sum(right, axis=1, keepdims=True), (1, 768))
+    pl.semaphore_wait(barrier, len(friends))
+
+    half = aligned(other, 384)
+    arrive = [
+        swap(0, at.key_w.at[:, half], at.come_a.at[:, pl.ds(0, 384)]),
+        swap(1, at.value_w.at[:, half], at.come_a.at[:, pl.ds(384, 384)]),
+        swap(2, at.query_w.at[:, half], at.come_b.at[:, pl.ds(0, 384)]),
+        swap(3, at.output_w.at[:, half], at.come_b.at[:, pl.ds(384, 384)]),
+        swap(4, at.table_t.at[:, aligned(other, 256)], at.come_b.at[:, pl.ds(768, 256)]),
+        swap(5, at.small, at.come_s),
+    ]
+    come_inner = swap(6, at.inner_w.at[other], at.come_1)
+    come_x = swap(7, at.hidden, at.x_all.at[own_rows])
+    place_x = pltpu.make_async_copy(at.hidden, at.x_all.at[own_rows], at.here.at[0])
+    place_x.start()
+    place_2 = pltpu.make_async_copy(at.outer_w, at.gat_2.at[r.z, r.plane], at.here.at[1])
+    place_2.start()
+    for copy in arrive:
+        copy.wait_recv()
+
+    def stack(mine, came):
+        mine, came = mine.astype(F32), came.astype(F32)
+        upper = jnp.where(core == 0, mine, came)
+        lower = jnp.where(core == 0, came, mine)
+        return low(jnp.concatenate([upper, lower], axis=0))
+
+    mine_half = aligned(core, 384)
+    at.gat_a[r.z, r.plane, :, 0:384] = stack(at.key_w[:, mine_half], at.come_a[:, 0:384])
+    at.gat_a[r.z, r.plane, :, 384:768] = stack(at.value_w[:, mine_half], at.come_a[:, 384:768])
+    at.gat_b[r.z, r.plane, :, 0:384] = stack(at.query_w[:, mine_half], at.come_b[:, 0:384])
+    at.gat_b[r.z, r.plane, :, 384:768] = stack(at.output_w[:, mine_half], at.come_b[:, 384:768])
+    at.gat_b[r.z, r.plane, :, 768:1024] = stack(
+        at.table_t[:, aligned(core, 256)], at.come_b[:, 768:1024]
+    )
+    at.gat_s[r.z, r.plane, core] = at.small[...]
+    at.gat_s[r.z, r.plane, other] = at.come_s[...]
+    gather_one.start()
+    come_inner.wait_recv()
+    at.gat_1[r.z, r.plane] = stack(at.inner_w[core], at.come_1[...])
+    place_2.wait()
+    place_x.wait()
+    come_x.wait_recv()
+    at.x_turned[...] = at.x_all[...].T
+    columns = lax.broadcasted_iota(jnp.int32, (512, 512), 1)
+    at.one_hot[...] = low((at.bucket_col[...] == columns).astype(F32))
+    flip_i = lax.broadcasted_iota(jnp.int32, (128, 128), 0)
+    flip_j = lax.broadcasted_iota(jnp.int32, (128, 128), 1)
+    at.flip[...] = low((flip_i + flip_j == 127).astype(F32))
+    for table in (at.near_rows, at.far_rows):
+        table[0:256, :] = jnp.zeros((256, 384), BF16)
+        table[768:1024, :] = jnp.zeros((256, 384), BF16)
+    for step in range(1, LINE):
+        gather_one.turn(step)
+    gather_one.corner(LINE - 1)
+    gather_two.start()
+    gather_one.finish()
+
+    out_mine = at.gat_b.at[:, :, :, pl.ds(384, 384)]
+    table_mine = at.gat_b.at[:, :, :, pl.ds(768, 256)]
+    come_table = swap(8, table_mine, at.table_all.at[core])
+    come_out = swap(9, out_mine, at.out_all.at[core])
+    place_table = pltpu.make_async_copy(table_mine, at.table_all.at[core], at.here.at[0])
+    place_table.start()
+    place_out = pltpu.make_async_copy(out_mine, at.out_all.at[core], at.here.at[1])
+    place_out.start()
+
+    for line in range(LINE):
+        for plane in range(4):
+            chip = line * 4 + plane
+            for which in range(2):
+                device = 2 * chip + which
+                tile = at.gat_s[line, plane, which].astype(F32)
+                at.vectors[:, 24 * device : 24 * device + 24] = tile[0:8, 0:24]
+            tile = at.gat_s[line, plane, core].astype(F32)
+            at.inner_bias[0:1, 96 * chip : 96 * chip + 96] = tile[8:9, 0:96]
+
+    def rows(value):
+        return value.reshape(768, value.shape[-1])
+
+    vector_half = aligned(core, 384)
+    query_bias = at.vectors[0:1, vector_half]
+    value_bias = at.vectors[1:2, vector_half]
+    at.kvq[:, 0:384] = low(dot(at.x_all[...], rows(at.gat_a[:, :, :, 0:384])))
+    at.kvq[:, 384:768] = low(dot(at.x_all[...], rows(at.gat_a[:, :, :, 384:768])) + value_bias)
+    at.kvq[:, 768:1152] = low(dot(at.x_all[...], rows(at.gat_b[:, :, :, 0:384])) + query_bias)
+    place_table.wait()
+    come_table.wait_recv()
+    for part in range(2):
+        piece = pl.ds(256 * part, 256)
+        table = rows(at.table_all[part])
+        at.key_rel[piece, :] = low(dot(table, rows(at.gat_a[:, :, :, 0:384]), 0, 0))
+        at.query_rel[piece, :] = low(dot(table, rows(at.gat_b[:, :, :, 0:384]), 0, 0) + query_bias)
+    at.near_rows[256:768, :] = low(dot(at.one_hot[...], at.key_rel[...]))
+    at.far_rows[256:768, :] = low(dot(at.one_hot[...], at.query_rel[...]))
+
+    gather_two.turn(1)
+
+    lanes = lax.broadcasted_iota(jnp.int32, (1, 128), 1) // HEAD
+    no_score = np.float32(NEGATIVE)
+
+    def forward_head(head):
+        pair = aligned(head // 2, 128)
+        key_lanes = pl.ds(pl.multiple_of((head // 2) * 128, 128), 128)
+        value_lanes = pl.ds(pl.multiple_of(384 + (head // 2) * 128, 128), 128)
+        query_lanes = pl.ds(pl.multiple_of(768 + (head // 2) * 128, 128), 128)
+        mine = lanes == head % 2
+        only = low(mine.astype(F32))
+        keys = at.kvq[:, key_lanes]
+        values = at.kvq[:, value_lanes]
+        for block in range(4):
+            piece = pl.ds(128 * block, 128)
+            shifted = dot(
+                at.kvq[piece, key_lanes] * only, at.far_rows[pl.ds(384 - 128 * block, 640), pair], 1, 1
+            )
+            at.far_scores[piece, :] = pltpu.roll(shifted, 0, 1, stride=1, stride_axis=0)[:, 128:640]
+        for block in range(4):
+            piece = pl.ds(128 * block, 128)
+            queries = at.kvq[piece, query_lanes] * only
+            shifted = dot(queries, at.near_rows[pl.ds(384 - 128 * block, 640), pair], 1, 1)
+            summed = (
+                dot(queries, keys, 1, 1)
+                + pltpu.roll(shifted, 0, 1, stride=1, stride_axis=0)[:, 128:640]
+                + at.far_scores[:, piece].T
+            )
+            masked = jnp.where(
+                at.segment_col[piece, :] == at.segment_row[...], summed * score_scale, no_score
+            )
+            highest = jnp.max(masked, axis=-1, keepdims=True)
+            expsum = jnp.exp(masked - highest)
+            soft = expsum / jnp.sum(expsum, axis=-1, keepdims=True)
+            at.soft[head, piece, :] = soft
+            context = dot(low(soft), values)
+            here = at.context.at[core, piece, pair]
+            here[...] = low(jnp.where(mine, context, here[...].astype(F32)))
+
+    def forward_pair(index):
+        loop(2, lambda which: forward_head(2 * index + which))
+        remote(
+            at.context.at[core, :, aligned(index, 128)],
+            at.context.at[core, :, aligned(index, 128)],
+            at.context_send.at[index],
+            at.context_recv.at[index],
+            r.partner,
+        ).start()
+
+    loop(3, forward_pair)
+    gather_two.turn(2)
+    place_out.wait()
+    come_out.wait_recv()
+    for index in range(3):
+        remote(
+            at.context.at[other, :, pl.ds(128 * index, 128)],
+            at.context.at[other, :, pl.ds(128 * index, 128)],
+            at.context_send.at[index],
+            at.context_recv.at[index],
+            r.partner,
+        ).wait_recv()
+
+    def vector(index):
+        return at.vectors[index : index + 1, :]
+
+    for part in range(2):
+        piece = pl.ds(384 * part, 384)
+        weight = rows(at.out_all[part])
+        at.wide[:, piece] = dot(at.context[0, own_rows, :], weight[0:384]) + dot(
+            at.context[1, own_rows, :], weight[384:768]
+        )
+
+    def first_norm(index):
+        piece = aligned(index, 64)
+        token_rows = pl.ds(pl.multiple_of(core * 256 + index * 64, 64), 64)
+        residual = at.x_all[token_rows, :].astype(F32) + at.wide[piece, :] + vector(2)
+        out, normed, inverse = norm(residual, vector(3), vector(4))
+        at.first_out[piece, :] = out
+        at.first_normed[piece, :] = normed
+        at.first_inverse[piece, :] = jnp.broadcast_to(inverse, (64, 128))
+        at.first_low[token_rows, :] = low(out)
+
+    loop(4, first_norm)
+    come_first = swap(10, at.first_low.at[own_rows], at.first_low.at[own_rows])
+    gather_two.turn(3)
+    come_first.wait_recv()
+    at.first_turned[...] = at.first_low[...].T
+    gather_two.corner(LINE - 1)
+    gather_two.finish()
+
+    def inner_units(index):
+        piece = aligned(index, 256)
+        pre = dot(at.first_low[...], rows(at.gat_1[:, :, :, piece])) + at.inner_bias[0:1, piece]
+        value, slope = erf_parts(pre)
+        at.active[:, piece] = low(value)
+        at.slope[:, piece] = slope
+
+    loop(6, inner_units)
+
+    def outer_half(rows_at, out):
+        for part in range(3):
+            piece = pl.ds(256 * part, 256)
+            out[:, piece] = dot(
+                at.active[rows_at, :], at.gat_2[:, :, :, piece].reshape(1536, 256)
+            )
+
+    outer_half(other_rows, at.part_send)
+    come_outer = swap(11, at.part_send, at.part_recv)
+    outer_half(own_rows, at.wide)
+    come_outer.wait_recv()
+
+    def second_norm(index):
+        piece = aligned(index, 64)
+        token_rows = pl.ds(pl.multiple_of(core * 256 + index * 64, 64), 64)
+        total = at.first_out[piece, :] + at.wide[piece, :] + at.part_recv[piece, :] + vector(5)
+        out, normed, inverse = norm(total, vector(6), vector(7))
+        at.result[piece, :] = low(out)
+        upstream = at.cotangent[piece, :].astype(F32)
+        grad = norm_pull(upstream, normed, inverse, vector(6))
+        at.grad_sum[piece, :] = grad
+        rounded = low(grad)
+        at.grad_outer[token_rows, :] = rounded
+        at.sums[5:6, :] += jnp.sum(rounded.astype(F32), axis=0, keepdims=True)
+        at.sums[6:7, :] += jnp.sum(upstream * normed, axis=0, keepdims=True)
+        at.sums[7:8, :] += jnp.sum(upstream, axis=0, keepdims=True)
+
+    loop(4, second_norm)
+    come_grad = swap(12, at.grad_outer.at[own_rows], at.grad_outer.at[own_rows])
+    scatter_two = Scatter(
+        r, (at.grad_1, at.grad_2), (at.one_1, at.one_2), (at.two_1, at.two_2),
+        (at.last_1, at.last_2), at.sf_send, at.sf_recv,
+    )
+    scatter_one = Scatter(
+        r, (at.grad_a, at.grad_b), (at.one_a, at.one_b), (at.two_a, at.two_b),
+        (at.last_a, at.last_b), at.sa_send, at.sa_recv,
+    )
+    come_grad.wait_recv()
+
+    def outer_weight(index):
+        units = aligned(index, 384)
+        grad = dot(at.active[:, units], at.grad_outer[...], 0, 0)
+        at.grad_2[index] = low(grad).reshape(4, 96, 768)
+
+    loop(4, outer_weight)
+    for step in (1, 2, 3, 0):
+        scatter_two.one(step, (1,))
+
+    def inner_grad(index):
+        units = aligned(index, 384)
+        grad = low(dot(at.grad_outer[...], at.gat_2[index].reshape(384, 768), 1, 1))
+        pre = low(grad.astype(F32) * at.slope[:, units])
+        at.grad_pre[:, units] = pre
+        at.bias_inner[0:1, units] = jnp.sum(pre.astype(F32), axis=0, keepdims=True)
+        at.grad_1[:, :, :, units] = low(dot(at.first_turned[...], pre)).reshape(LINE, 4, 48, 384)
+
+    loop(4, inner_grad)
+    for step in (1, 2, 3, 0):
+        scatter_two.one(step, (0,))
+    at.sums[8:9, :] = at.bias_inner[0:1, 0:768]
+    at.sums[9:10, :] = at.bias_inner[0:1, 768:1536]
+
+    def first_half(rows_at, out):
+        for part in range(2):
+            weight = at.gat_1[2 * part : 2 * part + 2].reshape(384, 1536)
+            out[:, 384 * part : 384 * part + 384] = dot(at.grad_pre[rows_at, :], weight, 1, 1)
+
+    first_half(other_rows, at.part_send2)
+    come_grad_first = swap(13, at.part_send2, at.part_recv2)
+    first_half(own_rows, at.wide)
+    come_grad_first.wait_recv()
+
+    def first_norm_back(index):
+        piece = aligned(index, 64)
+        token_rows = pl.ds(pl.multiple_of(core * 256 + index * 64, 64), 64)
+        upstream = at.wide[piece, :] + at.part_recv2[piece, :] + at.grad_sum[piece, :]
+        normed = at.first_normed[piece, :]
+        grad = norm_pull(upstream, normed, at.first_inverse[piece, 0:1], vector(3))
+        at.grad_sum[piece, :] = grad
+        rounded = low(grad)
+        at.grad_att[token_rows, :] = rounded
+        at.sums[2:3, :] += jnp.sum(rounded.astype(F32), axis=0, keepdims=True)
+        at.sums[3:4, :] += jnp.sum(upstream * normed, axis=0, keepdims=True)
+        at.sums[4:5, :] += jnp.sum(upstream, axis=0, keepdims=True)
+
+    loop(4, first_norm_back)
+    come_att = swap(14, at.grad_att.at[own_rows], at.grad_att.at[own_rows])
+    come_att.wait_recv()
+    scatter_two.two(1)
+    out_rows = pl.ds(pl.multiple_of(2 * core, 2), 2)
+    weight_0 = at.out_all[0, out_rows].reshape(384, 384)
+    weight_1 = at.out_all[1, out_rows].reshape(384, 384)
+    at.grad_context[...] = low(
+        dot(at.grad_att[:, 0:384], weight_0, 1, 1) + dot(at.grad_att[:, 384:768], weight_1, 1, 1)
+    )
+    for part in range(2):
+        grad = dot(at.context[part], at.grad_att[:, aligned(core, 384)], 0, 0)
+        at.grad_b[2 * part : 2 * part + 2, :, :, 384:768] = low(grad).reshape(2, 4, 48, 384)
+    scatter_two.two(2)
+
+    at.near_grad[...] = jnp.zeros_like(at.near_grad)
+    at.far_grad[...] = jnp.zeros_like(at.far_grad)
+    room = jnp.zeros((128, 128), BF16)
+
+    def spread(flipped):
+        return pltpu.roll(jnp.concatenate([flipped, room], axis=1), 1, 1, stride=1, stride_axis=0)
+
+    def backward_head(head):
+        pair = aligned(head // 2, 128)
+        key_lanes = pl.ds(pl.multiple_of((head // 2) * 128, 128), 128)
+        value_lanes = pl.ds(pl.multiple_of(384 + (head // 2) * 128, 128), 128)
+        query_lanes = pl.ds(pl.multiple_of(768 + (head // 2) * 128, 128), 128)
+        mine = lanes == head % 2
+        only = low(mine.astype(F32))
+        flip = at.flip[...]
+        keys = at.kvq[:, key_lanes]
+        queries = at.kvq[:, query_lanes]
+        values = at.kvq[:, value_lanes]
+
+        def merge(here, value):
+            here[...] = low(jnp.where(mine, value, here[...].astype(F32)))
+
+        for block in range(4):
+            piece = pl.ds(128 * block, 128)
+            window = pl.ds(384 - 128 * block, 640)
+            soft = at.soft[head, piece, :]
+            grad_soft = dot(at.grad_context[piece, pair] * only, values, 1, 1)
+            inner = jnp.sum(soft * grad_soft, axis=-1, keepdims=True)
+            grad_low = low(soft * (grad_soft - inner) * score_scale)
+            at.grad_low[piece, :] = grad_low
+            flipped = low(dot(flip, grad_low))
+            near = spread(flipped)
+            grad = low(dot(flipped, keys) + dot(near, at.near_rows[window, pair]))
+            merge(at.grad_kvq.at[piece, query_lanes], dot(flip, grad))
+            back = low(dot(flip, at.kvq[piece, query_lanes] * only))
+            at.near_grad[window, pair] += dot(near, back, 0, 0)
+        grad_context = at.grad_context[:, pair]
+        for block in range(4):
+            piece = pl.ds(128 * block, 128)
+            window = pl.ds(384 - 128 * block, 640)
+            flipped = low(dot(flip, at.grad_low[:, piece], 1, 1))
+            far = spread(flipped)
+            grad = low(dot(flipped, queries) + dot(far, at.far_rows[window, pair]))
+            merge(at.grad_kvq.at[piece, key_lanes], dot(flip, grad))
+            back = low(dot(flip, at.kvq[piece, key_lanes] * only))
+            at.far_grad[window, pair] += dot(far, back, 0, 0)
+            weights = low(at.soft[head, :, piece])
+            merge(at.grad_kvq.at[piece, value_lanes], dot(weights, grad_context, 0, 0))
+
+    def backward_pair(index):
+        loop(2, lambda which: backward_head(2 * index + which))
+        scatter_two.three(index + 1)
+
+        @pl.when(index < 2)
+        def _():
+            scatter_two.two(index + 3)
+
+    loop(3, backward_pair)
+    scatter_two.three(0, True)
+
+    grad_key_rel = dot(at.one_hot[...], low(at.near_grad[256:768, :]), 0, 0)
+    grad_query_rel = dot(at.one_hot[...], low(at.far_grad[256:768, :]), 0, 0)
+    at.key_rel[...] = low(grad_key_rel)
+    at.query_rel[...] = low(grad_query_rel)
+
+    def token_weight(kvq_at):
+        return dot(at.x_turned[...], at.grad_kvq[:, kvq_at : kvq_at + 384])
+
+    def table_weight(rel):
+        return dot(rows(at.table_all[0]), rel[0:256, :]) + dot(rows(at.table_all[1]), rel[256:512, :])
+
+    def shape_weight(value):
+        return low(value).reshape(LINE, 4, 48, value.shape[-1])
+
+    def table_half(which):
+        piece = aligned(which, 256)
+        return dot(rows(at.gat_b[:, :, :, 0:384]), at.query_rel[piece, :], 1, 1) + dot(
+            rows(at.gat_a[:, :, :, 0:384]), at.key_rel[piece, :], 1, 1
+        )
+
+    at.table_send[...] = shape_weight(table_half(other))
+    come_part = swap(15, at.table_send, at.table_recv)
+    at.grad_a[:, :, :, 0:384] = shape_weight(token_weight(0) + table_weight(at.key_rel))
+    at.grad_a[:, :, :, 384:768] = shape_weight(token_weight(384))
+    for step in (1, 2, 3, 0):
+        scatter_one.one(step, (0,))
+    at.grad_b[:, :, :, 0:384] = shape_weight(token_weight(768) + table_weight(at.query_rel))
+    own_table = table_half(core)
+    come_part.wait_recv()
+    at.grad_b[:, :, :, 768:1024] = shape_weight(own_table + rows(at.table_recv[...]).astype(F32))
+    for step in (1, 2, 3, 0):
+        scatter_one.one(step, (1,))
+
+    at.sums[0:1, vector_half] = jnp.sum(
+        at.grad_kvq[:, 768:1152].astype(F32), axis=0, keepdims=True
+    ) + jnp.sum(at.far_grad[256:768, :], axis=0, keepdims=True)
+    at.sums[1:2, vector_half] = jnp.sum(
+        at.grad_kvq[:, 384:768].astype(F32), axis=0, keepdims=True
+    )
+
+    def exchange(stage, source, device):
+        return remote(
+            source, at.sums_come.at[stage], at.sums_send.at[stage], at.sums_recv.at[stage], device
+        )
+
+    stage_copies = [exchange(0, at.sums, r.partner)]
+    stage_copies[0].start()
+
+    def input_half(rows_at, out):
+        for part in range(2):
+            weight_a = at.gat_a[2 * part : 2 * part + 2].reshape(384, 768)
+            weight_b = at.gat_b[2 * part : 2 * part + 2, :, :, 0:384].reshape(384, 384)
+            out[:, 384 * part : 384 * part + 384] = dot(
+                at.grad_kvq[rows_at, 0:768], weight_a, 1, 1
+            ) + dot(at.grad_kvq[rows_at, 768:1152], weight_b, 1, 1)
+
+    come_outer.wait_send()
+    input_half(other_rows, at.part_send)
+    come_input = swap(16, at.part_send, at.part_recv)
+
+    stage_copies[0].wait_recv()
+    lines = lax.broadcasted_iota(jnp.int32, (16, 1), 0)
+    shared = jnp.where((lines == 8) | (lines == 9), 0.0, at.sums_come[0])
+    at.sums_step[0] = at.sums[...] + shared
+    stage_copies.append(exchange(1, at.sums_step.at[0], r.at_x))
+    stage_copies[1].start()
+    scatter_one.two(1)
+    input_half(own_rows, at.wide)
+    scatter_one.two(2)
+    stage_copies[1].wait_recv()
+    at.sums_step[1] = at.sums_step[0] + at.sums_come[1]
+    stage_copies.append(exchange(2, at.sums_step.at[1], r.at_y))
+    stage_copies[2].start()
+    scatter_one.three(1)
+    scatter_one.two(3)
+    come_input.wait_recv()
+    at.input_grad[...] = low(at.grad_sum[...] + at.wide[...] + at.part_recv[...])
+
+    scatter_two.finish()
+    at.d_outer[...] = scatter_two.total(1)
+    inner_total = scatter_two.total(0)
+    at.give_1[...] = inner_total.reshape(2, 24, 1536)
+    swap(17, at.give_1.at[other], at.d_inner.at[core])
+    at.d_inner[core] = at.give_1[core]
+
+    scatter_one.three(2)
+    scatter_one.two(0)
+    stage_copies[2].wait_recv()
+    at.sums_step[2] = at.sums_step[1] + at.sums_come[2]
+    for step in range(1, LINE):
+        copy = exchange(2 + step, at.sums_step.at[2], r.at_line(r.ahead(step)))
+        copy.start()
+        stage_copies.append(copy)
+    scatter_one.three(3)
+    scatter_one.three(0, True)
+    for copy in stage_copies[3:]:
+        copy.wait_recv()
+    at.vector_grads[...] = (
+        at.sums_step[2] + at.sums_come[3] + at.sums_come[4] + at.sums_come[5]
+    )
+    scatter_one.finish()
+    at.give_a[...] = scatter_one.total(0).reshape(2, 24, 768)
+    at.give_b[...] = scatter_one.total(1).reshape(2, 24, 1024)
+    outs = (
+        (at.give_a, 0, 384, at.d_key),
+        (at.give_a, 384, 384, at.d_value),
+        (at.give_b, 0, 384, at.d_query),
+        (at.give_b, 384, 384, at.d_output),
+        (at.give_b, 768, 256, at.d_table),
+    )
+    for slot, (give, start, width, out) in enumerate(outs):
+        swap(18 + slot, give.at[other, :, pl.ds(start, width)], out.at[:, aligned(core, width)])
+        out[:, aligned(core, width)] = give[core, :, start : start + width]
+    for copy in waiting[17:]:
+        copy.wait_recv()
+    for copy in waiting:
+        if copy is not come_outer:
+            copy.wait_send()
+    for copy in stage_copies:
+        copy.wait_send()
+    for index in range(3):
+        remote(
+            at.context.at[core, :, pl.ds(128 * index, 128)],
+            at.context.at[core, :, pl.ds(128 * index, 128)],
+            at.context_send.at[index],
+            at.context_recv.at[index],
+            r.partner,
+        ).wait_send()
+    for user in (gather_one, gather_two, scatter_two, scatter_one):
+        user.sent()
+
+
+OUTPUTS = dict(
+    result=((256, 768), BF16),
+    input_grad=((256, 768), BF16),
+    d_query=((24, 768), F32),
+    d_key=((24, 768), F32),
+    d_value=((24, 768), F32),
+    d_output=((24, 768), F32),
+    d_table=((24, 512), F32),
+    d_inner=((2, 24, 1536), F32),
+    d_outer=((96, 768), F32),
+    vector_grads=((16, 768), F32),
+)
+LINE = 4
+BLOCKS = (LINE, 4, 48)
+SCRATCH = dict(
+    come_a=((24, 768), BF16),
+    come_b=((24, 1024), BF16),
+    come_s=((16, 128), BF16),
+    come_1=((24, 1536), BF16),
+    gat_a=(BLOCKS + (768,), BF16),
+    gat_b=(BLOCKS + (1024,), BF16),
+    gat_s=((LINE, 4, 2, 16, 128), BF16),
+    gat_1=(BLOCKS + (1536,), BF16),
+    gat_2=((LINE, 4, 96, 768), BF16),
+    x_all=((512, 768), BF16),
+    x_turned=((768, 512), BF16),
+    one_hot=((512, 512), BF16),
+    flip=((128, 128), BF16),
+    near_rows=((1024, 384), BF16),
+    far_rows=((1024, 384), BF16),
+    near_grad=((1024, 384), F32),
+    far_grad=((1024, 384), F32),
+    key_rel=((512, 384), BF16),
+    query_rel=((512, 384), BF16),
+    table_all=((2,) + BLOCKS + (256,), BF16),
+    out_all=((2,) + BLOCKS + (384,), BF16),
+    vectors=((8, 768), F32),
+    inner_bias=((8, 1536), F32),
+    bias_inner=((8, 1536), F32),
+    kvq=((512, 1152), BF16),
+    grad_kvq=((512, 1152), BF16),
+    far_scores=((512, 512), F32),
+    grad_low=((512, 512), BF16),
+    soft=((6, 512, 512), F32),
+    context=((2, 512, 384), BF16),
+    grad_context=((512, 384), BF16),
+    wide=((256, 768), F32),
+    first_out=((256, 768), F32),
+    first_normed=((256, 768), F32),
+    first_inverse=((256, 128), F32),
+    first_low=((512, 768), BF16),
+    first_turned=((768, 512), BF16),
+    active=((512, 1536), BF16),
+    slope=((512, 1536), F32),
+    grad_pre=((512, 1536), BF16),
+    part_send=((256, 768), F32),
+    part_recv=((256, 768), F32),
+    part_send2=((256, 768), F32),
+    part_recv2=((256, 768), F32),
+    grad_sum=((256, 768), F32),
+    grad_outer=((512, 768), BF16),
+    grad_att=((512, 768), BF16),
+    table_send=(BLOCKS + (256,), BF16),
+    table_recv=(BLOCKS + (256,), BF16),
+    sums=((16, 768), F32),
+    sums_step=((3, 16, 768), F32),
+    sums_come=((6, 16, 768), F32),
+    grad_1=(BLOCKS + (1536,), BF16),
+    grad_2=((LINE, 4, 96, 768), BF16),
+    one_1=((LINE, 2, 48, 1536), BF16),
+    one_2=((LINE, 2, 96, 768), BF16),
+    two_1=((LINE, 48, 1536), BF16),
+    two_2=((LINE, 96, 768), BF16),
+    last_1=((LINE, 48, 1536), BF16),
+    last_2=((LINE, 96, 768), BF16),
+    grad_a=(BLOCKS + (768,), BF16),
+    grad_b=(BLOCKS + (1024,), BF16),
+    one_a=((LINE, 2, 48, 768), BF16),
+    one_b=((LINE, 2, 48, 1024), BF16),
+    two_a=((LINE, 48, 768), BF16),
+    two_b=((LINE, 48, 1024), BF16),
+    last_a=((LINE, 48, 768), BF16),
+    last_b=((LINE, 48, 1024), BF16),
+    give_1=((2, 24, 1536), F32),
+    give_a=((2, 24, 768), F32),
+    give_b=((2, 24, 1024), F32),
+)
+SEMAPHORES = dict(
+    swap_send=(23,),
+    swap_recv=(23,),
+    here=(2,),
+    context_send=(3,),
+    context_recv=(3,),
+    ga_send=(3, 4, LINE),
+    ga_recv=(3, 4, LINE),
+    gf_send=(2, 4, LINE),
+    gf_recv=(2, 4, LINE),
+    sf_send=(2, 4, LINE),
+    sf_recv=(2, 4, LINE),
+    sa_send=(2, 4, LINE),
+    sa_recv=(2, 4, LINE),
+    sums_send=(6,),
+    sums_recv=(6,),
+)
+
+
+def block_shards(
+    hidden_in,
+    query_weight,
+    query_bias,
+    key_weight,
+    value_weight,
+    value_bias,
+    output_weight,
+    output_bias,
+    first_gain,
+    first_shift,
+    inner_weight,
+    inner_bias,
+    outer_weight,
+    outer_bias,
+    second_gain,
+    second_shift,
+    relative_table,
+    segments,
+    buckets,
+    predicted,
+    labels,
+    cotangent,
+):
+    chips = 4 * LINE
+    units = outer_weight.shape[0]
+    inner_pair = (
+        inner_weight.reshape(24, chips, 2, units).transpose(2, 0, 1, 3).reshape(2, 24, chips * units)
+    )
+    vectors = jnp.stack(
+        [
+            query_bias,
+            value_bias,
+            output_bias,
+            first_gain,
+            first_shift,
+            outer_bias,
+            second_gain,
+            second_shift,
+        ]
+    )
+    small = jnp.zeros((16, 128), BF16)
+    small = small.at[0:8, 0:24].set(vectors).at[8, 0:units].set(inner_bias)
+    inputs = dict(
+        hidden=hidden_in[0],
+        query_w=query_weight,
+        key_w=key_weight,
+        value_w=value_weight,
+        output_w=output_weight,
+        table_t=relative_table.T,
+        inner_w=inner_pair,
+        outer_w=outer_weight,
+        small=small,
+        segment_row=segments,
+        segment_col=segments.reshape(512, 1),
+        bucket_col=buckets[256:768][::-1].reshape(512, 1),
+        predicted=predicted,
+        labels=labels,
+        cotangent=cotangent[0],
+    )
+    names = tuple(inputs) + tuple(OUTPUTS) + tuple(SCRATCH) + tuple(SEMAPHORES)
+    vmem = pl.BlockSpec(memory_space=pltpu.VMEM)
+    outs = pl.pallas_call(
+        partial(layer_kernel, names),
+        name="layer",
+        out_shape=tuple(jax.ShapeDtypeStruct(*out) for out in OUTPUTS.values()),
+        in_specs=[vmem] * len(inputs),
+        out_specs=(vmem,) * len(OUTPUTS),
+        scratch_shapes=[pltpu.VMEM(*spec) for spec in SCRATCH.values()]
+        + [pltpu.SemaphoreType.DMA(shape) for shape in SEMAPHORES.values()],
+        compiler_params=pltpu.CompilerParams(
+            collective_id=0, has_side_effects=True, vmem_limit_bytes=67043328
+        ),
+    )(*inputs.values())
+    got = type("Outs", (), dict(zip(OUTPUTS, outs)))
+    chip = lax.axis_index("fsdp")
+    core = lax.axis_index("seq")
+    sums = got.vector_grads
+    own = lax.dynamic_slice(sums, (0, (2 * chip + core) * 24), (8, 24))
+    inner_bias_grad = lax.dynamic_slice(sums[8:10].reshape(1536), (chip * units,), (units,))
+    d_inner = (
+        got.d_inner.reshape(2, 24, chips, units).transpose(1, 2, 0, 3).reshape(24, 2 * chips * units)
+    )
+    return (
+        got.result[None],
+        got.input_grad[None],
+        got.d_query,
+        own[0],
+        got.d_key,
+        got.d_value,
+        own[1],
+        got.d_output,
+        own[2],
+        own[3],
+        own[4],
+        d_inner,
+        inner_bias_grad,
+        got.d_outer,
+        own[5],
+        own[6],
+        own[7],
+        got.d_table.T,
+        sums[10, 0].astype(jnp.int32),
+    )
+
+
+def fits(mesh):
+    return mesh.shape["fsdp"] == 4 * LINE and mesh.shape["seq"] == 2
+
+
 def solution(mesh):
     return jax.shard_map(
-        shards,
+        block_shards if fits(mesh) else shards,
         mesh=mesh,
         in_specs=(
             P("fsdp", "seq", None),

time: 1870 us -> 218 us (0.12)
  waiting for transfers between devices: 774 us -> 0 us
  local copies, waits for them, and re-layouts: 674 us -> 18.7 us
  Pallas kernels: 0 us -> 195 us
  blocking collectives: 171 us -> 0 us
  matrix products: 141 us -> 0 us
  loops' own time: 40.3 us -> 0 us
  other arithmetic: 36.6 us -> 0 us
    reduce_scatter x7 -> x0, waiting for transfers between devices: 581 us -> none  [the longest x1 142 us: shards(): lax.psum_scatter(inner_weight_part, ('fsdp', 'seq'), scatter_dimension=0,...]
    reshape x62 -> x8, local copies, waits for them, and re-layouts: 260 us -> 6.09 us  [the longest x2 2.34 us: block_shards(): got.d_inner.reshape(2, 24, chips, units).transpose(1, 2, 0, 3)]
    pallas_call x0 -> x1, Pallas kernels: none -> 195 us  [block_shards(): pl.pallas_call(partial(layer_kernel, names), name='layer', out_shape=tupl...]
    dot_general x114 -> x0, matrix products: 141 us -> none  [the longest x110 133 us: matmul(): return jnp.einsum(spec, left, right, preferred_element_type=jnp.float32)]
    dynamic_slice x97 -> x2, local copies, waits for them, and re-layouts: 140 us -> 1.36 us  [the longest x1 0.78 us: block_shards(): own = lax.dynamic_slice(sums, (0, (2 * chip + core) * 24), (8, 24))]
    unnamed x16 -> x0, waiting for transfers between devices: 109 us -> none
    unnamed x2 -> x0, blocking collectives: 84.2 us -> none
    while x198 -> x0, local copies, waits for them, and re-layouts: 69.5 us -> none
  transfers between devices with their start and end apart: 15 -> 0, of which waited for: 9 -> 0; matrix products, arithmetic and copies ran while one was open for 20% -> 0% of each run, Pallas kernels for 0% -> 0%
where the time goes in v1:
time: 218 us; the launch traced here: 216 us
  Pallas kernels  195 us (89%)
  local copies, waits for them, and re-layouts  18.7 us (9%)
  between operations  2.59 us (1%)
    pallas_call x1, Pallas kernels, block_shards(): pl.pallas_call(partial(layer_kernel, names), name='layer', out_shape=tupl...  195 us
    unnamed x48, local copies, waits for them, and re-layouts  8.24 us

profile of v1, /device:TPU:0, one launch (start us, length us, event | category | flops | bytes accessed | tf_op | source)
XLA Modules:
  0.0 216.4 jit_solution(10039842105262123177)
XLA Ops:
  0.7 1.1 reshape.120
  1.8 0.9 reshape.121.refs_6_
  2.7 0.0 copy-start.14
  2.7 0.0 copy-start.15
  2.7 0.0 copy-start.16
  2.7 0.0 copy-start.17
  2.7 0.0 copy-start.18
  2.7 0.0 copy-start.11
  2.7 0.0 copy-start.12
  2.7 0.0 copy-start.13
  2.8 0.6 copy-done.14
  3.3 0.0 copy-done.15
  3.4 0.0 copy-done.16
  3.4 0.0 copy-done.17
  3.4 0.0 copy-done.18
  3.4 0.0 copy-done.11
  3.4 0.0 copy-done.12
  3.4 0.0 copy-done.13
  3.5 0.0 copy-start.19
  3.5 0.6 copy-done.19
  4.2 0.0 copy-start.9
  4.2 0.1 scatter.9.refs_8_
  4.2 0.0 copy-start.8
  4.3 0.6 copy-done.9
  4.8 0.0 copy-start.10
  4.8 0.9 copy.44.refs_10_
  5.7 0.0 copy-done.8
  5.7 0.0 copy-done.10
  5.7 0.1 rev.3
  5.8 0.9 copy.45.refs_11_
  6.7 195.1 %layer.1 = (bf16[256,768]{1,0:T(8,128)(2,1)}, bf16[256,768]{1,0:T(8,128)(2,1)}, f32[24,768]{1,0:T(8,128)}, f32[24,768]{1,0:T(8,128)}, f32[24,768]{1,0:T(8,128)},...) custom-call(bf16[256,768]{1,0:T(8,128)(2,1)} %bitcast.42, ...), custom_call_target="tpu_custom_call" | custom-call | tf_op jit(solution)/shard_map/layer/pallas_call | solution.py:1367
  201.8 0.8 constant_dynamic-slice_fusion
  202.6 0.5 slice_bitcast_fusion
  203.2 1.1 reshape.125
  204.3 0.3 copy.46
  204.6 0.0 copy-start.1
  204.6 1.2 reshape.126
  205.8 0.7 slice.78
  206.6 0.6 dynamic_slice.7
  207.2 1.2 slice.82
  209.0 0.0 copy-done.1
  209.0 0.0 copy-start
  209.0 0.7 copy.58
  209.8 0.4 copy-done
  210.2 0.0 copy-start.6
  210.2 0.0 copy-start.5
  210.2 0.0 copy-start.4
  210.2 0.7 copy.59
  210.9 0.2 copy-done.6
  211.1 0.0 copy-start.2
  211.1 0.6 copy.60
  211.7 0.0 copy-done.5
  211.7 0.6 copy.61
  212.3 0.0 copy-done.4
  212.3 0.0 copy-start.3
  212.3 0.6 copy.62
  213.0 0.3 copy-done.3
  213.3 0.6 copy.63
  213.9 0.0 copy-done.2
  213.9 0.0 copy-start.7
  213.9 0.7 copy.64
  214.6 0.1 copy-done.7
  214.7 0.6 copy.65
  (5 shorter events, 0.1 us)
Async XLA Ops:
  2.7 0.7 copy-start.14
  2.7 0.7 copy-start.15
  2.7 0.7 copy-start.16
  2.7 0.7 copy-start.17
  2.7 0.7 copy-start.18
  2.7 0.7 copy-start.11
  2.7 0.7 copy-start.12
  2.7 0.7 copy-start.13
  3.5 0.7 copy-start.19
  4.2 0.7 copy-start.9
  4.2 1.5 copy-start.8
  4.8 0.9 copy-start.10
  204.6 4.4 %copy-start.1 = (bf16[256,768]{1,0:T(8,128)(2,1)S(1)}, bf16[256,768]{1,0:T(8,128)(2,1)}, u32[]{:S(2)}) copy-start(bf16[256,768]{1,0:T(8,128)(2,1)} %get-tuple-element.53) | copy-start | bytes 1179652
  209.0 1.1 copy-start
  210.2 0.9 copy-start.6
  210.2 1.5 copy-start.5
  210.2 2.2 %copy-start.4 = (f32[24,768]{1,0:T(8,128)S(1)}, f32[24,768]{1,0:T(8,128)}, u32[]{:S(2)}) copy-start(f32[24,768]{1,0:T(8,128)} %get-tuple-element.95) | copy-start | bytes 221188
  211.1 2.8 %copy-start.2 = (f32[96,768]{1,0:T(8,128)S(1)}, f32[96,768]{1,0:T(8,128)}, u32[]{:S(2)}) copy-start(f32[96,768]{1,0:T(8,128)} %get-tuple-element.103) | copy-start | bytes 884740
  212.3 0.9 copy-start.3
  213.9 0.8 copy-start.7

commit v2 on v1

--- a/solution.py
+++ b/solution.py
@@ -707,6 +707,14 @@
     gather_two = Gather(r, (at.gat_1, at.gat_2), at.gf_send, at.gf_recv)
 
     at.sums[...] = jnp.zeros_like(at.sums)
+    at.small_wide[...] = jnp.zeros_like(at.small_wide)
+    small_rows = (
+        at.query_b, at.value_b, at.output_b, at.gain_1, at.shift_1, at.outer_b, at.gain_2, at.shift_2,
+        at.inner_b,
+    )
+    for index, row in enumerate(small_rows):
+        at.small_wide[index : index + 1, 0 : row.shape[1]] = row[...].astype(F32)
+    at.small[...] = low(at.small_wide[...])
     right = (at.predicted[...] == at.labels[...]).astype(F32)
     at.sums[10:11, :] = jnp.broadcast_to(jnp.sum(right, axis=1, keepdims=True), (1, 768))
     pl.semaphore_wait(barrier, len(friends))
@@ -720,7 +728,6 @@
         swap(4, at.table_t.at[:, aligned(other, 256)], at.come_b.at[:, pl.ds(768, 256)]),
         swap(5, at.small, at.come_s),
     ]
-    come_inner = swap(6, at.inner_w.at[other], at.come_1)
     come_x = swap(7, at.hidden, at.x_all.at[own_rows])
     place_x = pltpu.make_async_copy(at.hidden, at.x_all.at[own_rows], at.here.at[0])
     place_x.start()
@@ -746,14 +753,26 @@
     at.gat_s[r.z, r.plane, core] = at.small[...]
     at.gat_s[r.z, r.plane, other] = at.come_s[...]
     gather_one.start()
+    for chip in range(4 * LINE):
+        for which in range(2):
+            device = 2 * chip + which
+            at.inner_pair[which, :, 96 * chip : 96 * chip + 96] = at.inner_w[
+                :, 96 * device : 96 * device + 96
+            ]
+    come_inner = swap(6, at.inner_pair.at[other], at.come_1)
     come_inner.wait_recv()
-    at.gat_1[r.z, r.plane] = stack(at.inner_w[core], at.come_1[...])
+    at.gat_1[r.z, r.plane] = stack(at.inner_pair[core], at.come_1[...])
     place_2.wait()
     place_x.wait()
     come_x.wait_recv()
     at.x_turned[...] = at.x_all[...].T
-    columns = lax.broadcasted_iota(jnp.int32, (512, 512), 1)
-    at.one_hot[...] = low((at.bucket_col[...] == columns).astype(F32))
+    wide_i = lax.broadcasted_iota(jnp.int32, (512, 512), 0)
+    wide_j = lax.broadcasted_iota(jnp.int32, (512, 512), 1)
+    used = low((at.buckets[0:1, 256:768] == wide_i).astype(F32))
+    at.one_hot[...] = low(dot(used, low((wide_i + wide_j == 511).astype(F32))))
+    segment_wide = jnp.broadcast_to(at.segments[...].astype(F32), (128, 512))
+    at.segment_row[...] = segment_wide[0:8]
+    at.segment_col[...] = segment_wide.T
     flip_i = lax.broadcasted_iota(jnp.int32, (128, 128), 0)
     flip_j = lax.broadcasted_iota(jnp.int32, (128, 128), 1)
     at.flip[...] = low((flip_i + flip_j == 127).astype(F32))
@@ -801,8 +820,8 @@
         table = rows(at.table_all[part])
         at.key_rel[piece, :] = low(dot(table, rows(at.gat_a[:, :, :, 0:384]), 0, 0))
         at.query_rel[piece, :] = low(dot(table, rows(at.gat_b[:, :, :, 0:384]), 0, 0) + query_bias)
-    at.near_rows[256:768, :] = low(dot(at.one_hot[...], at.key_rel[...]))
-    at.far_rows[256:768, :] = low(dot(at.one_hot[...], at.query_rel[...]))
+    at.near_rows[256:768, :] = low(dot(at.one_hot[...], at.key_rel[...], 0, 0))
+    at.far_rows[256:768, :] = low(dot(at.one_hot[...], at.query_rel[...], 0, 0))
 
     gather_two.turn(1)
 
@@ -834,7 +853,7 @@
                 + at.far_scores[:, piece].T
             )
             masked = jnp.where(
-                at.segment_col[piece, :] == at.segment_row[...], summed * score_scale, no_score
+                at.segment_col[piece, 0:1] == at.segment_row[0:1, :], summed * score_scale, no_score
             )
             highest = jnp.max(masked, axis=-1, keepdims=True)
             expsum = jnp.exp(masked - highest)
@@ -1064,8 +1083,8 @@
     loop(3, backward_pair)
     scatter_two.three(0, True)
 
-    grad_key_rel = dot(at.one_hot[...], low(at.near_grad[256:768, :]), 0, 0)
-    grad_query_rel = dot(at.one_hot[...], low(at.far_grad[256:768, :]), 0, 0)
+    grad_key_rel = dot(at.one_hot[...], low(at.near_grad[256:768, :]))
+    grad_query_rel = dot(at.one_hot[...], low(at.far_grad[256:768, :]))
     at.key_rel[...] = low(grad_key_rel)
     at.query_rel[...] = low(grad_query_rel)
 
@@ -1196,6 +1215,37 @@
         user.sent()
 
 
+def finish_kernel(names, *refs):
+    at = type("Refs", (), dict(zip(names, refs)))
+    chip, core = lax.axis_index("fsdp"), lax.axis_index("seq")
+    at.result_out[...] = at.result[...]
+    at.input_grad_out[...] = at.input_grad[...]
+    at.query_w_out[...] = at.d_query[...]
+    at.key_w_out[...] = at.d_key[...]
+    at.value_w_out[...] = at.d_value[...]
+    at.output_w_out[...] = at.d_output[...]
+    at.table_out[...] = at.d_table[...]
+    at.outer_w_out[...] = at.d_outer[...]
+    for group in range(4 * LINE):
+        for which in range(2):
+            device = 2 * group + which
+            at.inner_w_out[:, 96 * device : 96 * device + 96] = at.d_inner[
+                which, :, 96 * group : 96 * group + 96
+            ]
+    sums = at.vector_grads[...]
+    own = pltpu.roll(sums, (768 - 24 * (2 * chip + core)) % 768, 1)
+    small_outs = (
+        at.query_b_out, at.value_b_out, at.output_b_out, at.gain_1_out, at.shift_1_out,
+        at.outer_b_out, at.gain_2_out, at.shift_2_out,
+    )
+    for index, out in enumerate(small_outs):
+        out[...] = own[index : index + 1, 0:24]
+    units = jnp.where(chip < 2 * LINE, sums[8:9], sums[9:10])
+    units = jnp.broadcast_to(units, (8, 768))
+    at.inner_b_out[...] = pltpu.roll(units, (768 - 96 * (chip % (2 * LINE))) % 768, 1)[0:1, 0:96]
+    at.count_out[...] = sums[10:11, 0:1].astype(jnp.int32)
+
+
 OUTPUTS = dict(
     result=((256, 768), BF16),
     input_grad=((256, 768), BF16),
@@ -1208,9 +1258,35 @@
     d_outer=((96, 768), F32),
     vector_grads=((16, 768), F32),
 )
+FINALS = dict(
+    result_out=((256, 768), BF16),
+    input_grad_out=((256, 768), BF16),
+    query_w_out=((24, 768), F32),
+    key_w_out=((24, 768), F32),
+    value_w_out=((24, 768), F32),
+    output_w_out=((24, 768), F32),
+    table_out=((24, 512), F32),
+    inner_w_out=((24, 3072), F32),
+    outer_w_out=((96, 768), F32),
+    query_b_out=((1, 24), F32),
+    value_b_out=((1, 24), F32),
+    output_b_out=((1, 24), F32),
+    gain_1_out=((1, 24), F32),
+    shift_1_out=((1, 24), F32),
+    outer_b_out=((1, 24), F32),
+    gain_2_out=((1, 24), F32),
+    shift_2_out=((1, 24), F32),
+    inner_b_out=((1, 96), F32),
+    count_out=((1, 1), jnp.int32),
+)
 LINE = 4
 BLOCKS = (LINE, 4, 48)
 SCRATCH = dict(
+    small_wide=((16, 128), F32),
+    small=((16, 128), BF16),
+    inner_pair=((2, 24, 1536), BF16),
+    segment_row=((8, 512), F32),
+    segment_col=((512, 128), F32),
     come_a=((24, 768), BF16),
     come_b=((24, 1024), BF16),
     come_s=((16, 128), BF16),
@@ -1326,25 +1402,6 @@
     labels,
     cotangent,
 ):
-    chips = 4 * LINE
-    units = outer_weight.shape[0]
-    inner_pair = (
-        inner_weight.reshape(24, chips, 2, units).transpose(2, 0, 1, 3).reshape(2, 24, chips * units)
-    )
-    vectors = jnp.stack(
-        [
-            query_bias,
-            value_bias,
-            output_bias,
-            first_gain,
-            first_shift,
-            outer_bias,
-            second_gain,
-            second_shift,
-        ]
-    )
-    small = jnp.zeros((16, 128), BF16)
-    small = small.at[0:8, 0:24].set(vectors).at[8, 0:units].set(inner_bias)
     inputs = dict(
         hidden=hidden_in[0],
         query_w=query_weight,
@@ -1352,12 +1409,19 @@
         value_w=value_weight,
         output_w=output_weight,
         table_t=relative_table.T,
-        inner_w=inner_pair,
+        inner_w=inner_weight,
         outer_w=outer_weight,
-        small=small,
-        segment_row=segments,
-        segment_col=segments.reshape(512, 1),
-        bucket_col=buckets[256:768][::-1].reshape(512, 1),
+        query_b=query_bias[None],
+        value_b=value_bias[None],
+        output_b=output_bias[None],
+        gain_1=first_gain[None],
+        shift_1=first_shift[None],
+        outer_b=outer_bias[None],
+        gain_2=second_gain[None],
+        shift_2=second_shift[None],
+        inner_b=inner_bias[None],
+        segments=segments,
+        buckets=buckets[None],
         predicted=predicted,
         labels=labels,
         cotangent=cotangent[0],
@@ -1376,35 +1440,34 @@
             collective_id=0, has_side_effects=True, vmem_limit_bytes=67043328
         ),
     )(*inputs.values())
-    got = type("Outs", (), dict(zip(OUTPUTS, outs)))
-    chip = lax.axis_index("fsdp")
-    core = lax.axis_index("seq")
-    sums = got.vector_grads
-    own = lax.dynamic_slice(sums, (0, (2 * chip + core) * 24), (8, 24))
-    inner_bias_grad = lax.dynamic_slice(sums[8:10].reshape(1536), (chip * units,), (units,))
-    d_inner = (
-        got.d_inner.reshape(2, 24, chips, units).transpose(1, 2, 0, 3).reshape(24, 2 * chips * units)
-    )
+    finals = pl.pallas_call(
+        partial(finish_kernel, tuple(OUTPUTS) + tuple(FINALS)),
+        name="finish",
+        out_shape=tuple(jax.ShapeDtypeStruct(*out) for out in FINALS.values()),
+        in_specs=[vmem] * len(OUTPUTS),
+        out_specs=(vmem,) * len(FINALS),
+    )(*outs)
+    got = type("Outs", (), dict(zip(FINALS, finals)))
     return (
-        got.result[None],
-        got.input_grad[None],
-        got.d_query,
-        own[0],
-        got.d_key,
-        got.d_value,
-        own[1],
-        got.d_output,
-        own[2],
-        own[3],
-        own[4],
-        d_inner,
-        inner_bias_grad,
-        got.d_outer,
-        own[5],
-        own[6],
-        own[7],
-        got.d_table.T,
-        sums[10, 0].astype(jnp.int32),
+        got.result_out[None],
+        got.input_grad_out[None],
+        got.query_w_out,
+        got.query_b_out[0],
+        got.key_w_out,
+        got.value_w_out,
+        got.value_b_out[0],
+        got.output_w_out,
+        got.output_b_out[0],
+        got.gain_1_out[0],
+        got.shift_1_out[0],
+        got.inner_w_out,
+        got.inner_b_out[0],
+        got.outer_w_out,
+        got.outer_b_out[0],
+        got.gain_2_out[0],
+        got.shift_2_out[0],
+        got.table_out.T,
+        got.count_out[0, 0],
     )
 
 

time: 218 us -> 200 us (0.917)
  local copies, waits for them, and re-layouts: 18.7 us -> 0 us
  Pallas kernels: 195 us -> 198 us
    unnamed x48 -> x0, local copies, waits for them, and re-layouts: 8.24 us -> none
    reshape x8 -> x0, local copies, waits for them, and re-layouts: 6.09 us -> none  [the longest x2 2.34 us: block_shards(): got.d_inner.reshape(2, 24, chips, units).transpose(1, 2, 0, 3)]
    pallas_call x0 -> x1, Pallas kernels: none -> 2.83 us  [block_shards(): pl.pallas_call(partial(finish_kernel, tuple(OUTPUTS) + tuple(FINALS)), na...]
where the time goes in v2:
time: 200 us; the launch traced here: 199 us
  Pallas kernels  198 us (99%)
    pallas_call x1, Pallas kernels, block_shards(): pl.pallas_call(partial(layer_kernel, names), name='layer', out_shape=tupl...  195 us

profile of v2, /device:TPU:0, one launch (start us, length us, event | category | flops | bytes accessed | tf_op | source)
XLA Modules:
  0.0 198.8 jit_solution(15590999978324391866)
XLA Ops:
  0.7 195.2 %layer.1 = (bf16[256,768]{1,0:T(8,128)(2,1)}, bf16[256,768]{1,0:T(8,128)(2,1)}, f32[24,768]{1,0:T(8,128)}, f32[24,768]{1,0:T(8,128)}, f32[24,768]{1,0:T(8,128)},...) custom-call(bf16[256,768]{1,0:T(8,128)(2,1)} %bitcast.26, ...), custom_call_target="tpu_custom_call" | custom-call | tf_op jit(solution)/shard_map/layer/pallas_call | solution.py:1431
  195.9 2.8 %finish.1 = (bf16[256,768]{1,0:T(8,128)(2,1)}, bf16[256,768]{1,0:T(8,128)(2,1)}, f32[24,768]{1,0:T(8,128)}, f32[24,768]{1,0:T(8,128)}, f32[24,768]{1,0:T(8,128)}...) custom-call(bf16[256,768]{1,0:T(8,128)(2,1)} %get-tuple-element.48.r, ...), custom_call_target="tpu_custom_call" | custom-call | tf_op jit(solution)/shard_map/finish/pallas_call | solution.py:1443

commit v3 on v2

--- a/solution.py
+++ b/solution.py
@@ -423,6 +423,9 @@
         self.plane = chip % 4
         self.plane_x = self.plane + 1 - 2 * self.x
         self.plane_y = self.plane + 2 - 4 * self.y
+        self.pair = self.z + 1 - 2 * (self.z % 2)
+        self.near = (self.z, (self.z + 2) % LINE)
+        self.far = (self.pair, (self.pair + 2) % LINE)
         self.partner = (chip, self.other)
         self.at_x = (self.z * 4 + self.plane_x, self.core)
         self.at_y = (self.z * 4 + self.plane_y, self.core)
@@ -447,203 +450,215 @@
     def __init__(self, route, arrays, send, recv):
         self.r, self.arrays, self.send, self.recv = route, arrays, send, recv
 
-    def copy(self, which, kind, send_at, recv_at, line, plane, device):
-        block = self.arrays[which].at[line, plane]
+    def copies(self, kind, line):
+        r = self.r
+        for i, array in enumerate(self.arrays):
+            by_x = i == 1
+            plane, device = (
+                (r.plane, r.at_line((r.z + 1) % LINE)),
+                (r.plane, r.at_line((r.z + LINE - 1) % LINE)),
+                (r.plane, r.at_x),
+                (r.plane, r.at_y),
+                (r.plane_y, r.at_x) if by_x else (r.plane_x, r.at_y),
+                (3 - r.plane, r.at_line(r.pair)),
+            )[kind]
+            block = array.at[line, plane]
+            yield remote(
+                block, block, self.send.at[i, kind, line], self.recv.at[i, kind, line], device
+            )
+
+    def begin(self, kind, line):
+        for copy in self.copies(kind, line):
+            copy.start()
+
+    def got(self, kind, line):
+        for copy in self.copies(kind, line):
+            copy.wait_recv()
+
+    def sides(self, line):
+        self.begin(2, line)
+        self.begin(3, line)
+
+    def got_sides(self, line):
+        self.got(2, line)
+        self.got(3, line)
+
+    def up(self, line):
+        @pl.when(self.r.z < LINE - 1)
+        def _():
+            self.begin(0, line)
+
+    def down(self, line):
+        @pl.when(self.r.z > 0)
+        def _():
+            self.begin(1, line)
+
+    def start_line(self):
+        self.up(self.r.z)
+        self.down(self.r.z)
+
+    def start_sides(self):
+        self.sides(self.r.z)
+
+    def round(self, step):
+        r = self.r
+
+        @pl.when(r.z >= step)
+        def _():
+            self.got(0, r.z - step)
+            self.up(r.z - step)
+            self.sides(r.z - step)
+
+        @pl.when(r.z + step < LINE)
+        def _():
+            self.got(1, r.z + step)
+            self.down(r.z + step)
+            self.sides(r.z + step)
+
+    def corner(self, which):
+        line = self.r.near[which]
+        self.got_sides(line)
+        self.begin(4, line)
+
+    def hand(self, which):
+        line = self.r.near[which]
+        self.got(4, line)
+        self.begin(5, line)
+
+    def finish(self):
+        for line in self.r.far:
+            self.got_sides(line)
+            self.got(5, line)
+
+    def drained(self, kind, line):
+        for copy in self.copies(kind, line):
+            copy.wait_send()
+
+    def sent(self):
+        r = self.r
+        for line in range(LINE):
+
+            @pl.when((r.z < LINE - 1) & (r.z >= line))
+            def _():
+                self.drained(0, line)
+
+            @pl.when((r.z > 0) & (r.z <= line))
+            def _():
+                self.drained(1, line)
+
+            self.drained(2, line)
+            self.drained(3, line)
+        for line in r.near:
+            self.drained(4, line)
+            self.drained(5, line)
+
+
+class Scatter:
+    def __init__(self, route, arrays, rooms, send, recv):
+        self.r, self.arrays, self.rooms = route, arrays, rooms
+        self.send, self.recv = send, recv
+
+    def across(self, i):
+        return self.r.plane_y if i == 0 else self.r.plane_x
+
+    def copy(self, i, kind, line):
+        r = self.r
+        near, across = (r.at_x, r.at_y) if i == 0 else (r.at_y, r.at_x)
+        near_plane = r.plane_x if i == 0 else r.plane_y
+        plane, room, device = (
+            (3 - r.plane, line // 2, r.at_line(r.pair)),
+            (near_plane, line, near),
+            (3 - r.plane, line // 2, near),
+            (self.across(i), line, across),
+            (r.plane, r.z, r.at_line(line)),
+        )[kind]
         return remote(
-            block,
-            block,
-            self.send.at[which, kind, send_at],
-            self.recv.at[which, kind, recv_at],
+            self.arrays[i].at[line, plane],
+            self.rooms[i][kind].at[room],
+            self.send.at[i, kind, line],
+            self.recv.at[i, kind, r.z if kind == 4 else line],
             device,
         )
 
-    def along_line(self, step):
+    def got_along(self, i, line):
         r = self.r
-        return [
-            self.copy(i, 0, step, r.z, r.z, r.plane, r.at_line(r.ahead(step)))
-            for i in range(len(self.arrays))
-        ]
-
-    def to_sides(self, line):
-        r = self.r
-        return [
-            self.copy(i, kind, line, line, line, r.plane, device)
-            for i in range(len(self.arrays))
-            for kind, device in ((1, r.at_x), (2, r.at_y))
-        ]
-
-    def to_corner(self, line):
-        r = self.r
-        return [
-            self.copy(
-                i,
-                3,
-                line,
-                line,
-                line,
-                r.plane_y if i == 1 else r.plane_x,
-                r.at_x if i == 1 else r.at_y,
-            )
-            for i in range(len(self.arrays))
-        ]
-
-    def start(self):
-        for step in range(1, LINE):
-            for copy in self.along_line(step):
-                copy.start()
-        for copy in self.to_sides(self.r.z):
-            copy.start()
-
-    def got_line(self, step):
-        r = self.r
-        line = r.behind(step)
-        for i in range(len(self.arrays)):
-            self.copy(i, 0, step, line, line, r.plane, r.at_line(line)).wait_recv()
-
-    def got_sides(self, line):
-        r = self.r
-        for i in range(len(self.arrays)):
-            self.copy(i, 1, line, line, line, r.plane_x, r.at_x).wait_recv()
-            self.copy(i, 2, line, line, line, r.plane_y, r.at_y).wait_recv()
-
-    def got_corner(self, line):
-        r = self.r
-        for i in range(len(self.arrays)):
-            self.copy(i, 3, line, line, line, 3 - r.plane, r.at_y).wait_recv()
-
-    def turn(self, step):
-        self.got_line(step)
-        for copy in self.to_sides(self.r.behind(step)):
-            copy.start()
-        self.corner(step - 1)
-
-    def corner(self, step):
-        line = self.r.behind(step) if step else self.r.z
-        self.got_sides(line)
-        for copy in self.to_corner(line):
-            copy.start()
-
-    def finish(self):
-        for line in range(LINE):
-            self.got_corner(line)
-
-    def sent(self):
-        for step in range(1, LINE):
-            for copy in self.along_line(step):
-                copy.wait_send()
-        for line in range(LINE):
-            for copy in self.to_sides(line) + self.to_corner(line):
-                copy.wait_send()
-
-
-class Scatter:
-    def __init__(self, route, arrays, first, second, last, send, recv):
-        self.r, self.arrays = route, arrays
-        self.first, self.second, self.last = first, second, last
-        self.send, self.recv = send, recv
-
-    def side(self, i, k):
-        r = self.r
-        return (1 - r.x) + 2 * k if i == 0 else 2 * (1 - r.y) + k
-
-    def kept(self, i, k):
-        r = self.r
-        return r.x + 2 * k if i == 0 else 2 * r.y + k
-
-    def step_one(self, line, which=(0, 1)):
-        r = self.r
-        return [
-            remote(
-                self.arrays[i].at[line, self.side(i, k)],
-                self.first[i].at[line, k],
-                self.send.at[i, k, line],
-                self.recv.at[i, k, line],
-                r.at_x if i == 0 else r.at_y,
-            )
-            for i in which
-            for k in (0, 1)
-        ]
-
-    def step_two(self, line):
-        r = self.r
-        return [
-            remote(
-                self.arrays[i].at[line, r.plane_y if i == 0 else r.plane_x],
-                self.second[i].at[line],
-                self.send.at[i, 2, line],
-                self.recv.at[i, 2, line],
-                r.at_y if i == 0 else r.at_x,
-            )
-            for i in (0, 1)
-        ]
-
-    def step_line(self, step):
-        r = self.r
-        line = r.ahead(step)
-        return [
-            remote(
-                self.arrays[i].at[line, r.plane],
-                self.last[i].at[r.z],
-                self.send.at[i, 3, step],
-                self.recv.at[i, 3, r.z],
-                r.at_line(line),
-            )
-            for i in (0, 1)
-        ]
-
-    def one(self, step, which=(0, 1)):
-        for copy in self.step_one(self.r.ahead(step), which):
-            copy.start()
-
-    def two(self, step):
-        line = self.r.ahead(step)
-        for copy in self.step_one(line):
-            copy.wait_recv()
-        for i in (0, 1):
-            for k in (0, 1):
-                at = self.arrays[i].at[line, self.kept(i, k)]
-                at[...] = low(at[...].astype(F32) + self.first[i][line, k].astype(F32))
-        for copy in self.step_two(line):
-            copy.start()
-
-    def three(self, step, last=False):
-        line = self.r.ahead(step)
-        for copy in self.step_two(line):
-            copy.wait_recv()
-        for i in (0, 1):
-            at = self.arrays[i].at[line, self.r.plane]
-            at[...] = low(at[...].astype(F32) + self.second[i][line].astype(F32))
-        if not last:
-            for copy in self.step_line(step):
-                copy.start()
+        remote(
+            self.arrays[i].at[line, r.plane],
+            self.rooms[i][4].at[line],
+            self.send.at[i, 4, line],
+            self.recv.at[i, 4, line],
+            r.at_line(line),
+        ).wait_recv()
+
+    def begin_far(self, i, line):
+        for kind in (0, 1, 3):
+            self.copy(i, kind, line).start()
+
+    def begin_near(self, i, line):
+        self.copy(i, 1, line).start()
+
+    def begin(self, i):
+        for line in self.r.far:
+            self.begin_far(i, line)
+        for line in self.r.near[::-1]:
+            self.begin_near(i, line)
+
+    def merge(self, i, line, plane, *came):
+        at = self.arrays[i].at[line, plane]
+        value = at[...].astype(F32)
+        for kind, room in came:
+            value = value + self.rooms[i][kind][room].astype(F32)
+        at[...] = low(value)
+
+    def corners(self, i):
+        for line in self.r.near[::-1]:
+            self.copy(i, 0, line).wait_recv()
+            self.merge(i, line, 3 - self.r.plane, (0, line // 2))
+            self.copy(i, 2, line).start()
+
+    def turn(self, i):
+        for line in self.r.near[::-1]:
+            self.copy(i, 2, line).wait_recv()
+            self.merge(i, line, self.across(i), (2, line // 2))
+            self.copy(i, 3, line).start()
+
+    def along(self, i, line):
+        self.copy(i, 1, line).wait_recv()
+        self.copy(i, 3, line).wait_recv()
+        self.merge(i, line, self.r.plane, (1, line), (3, line))
+        self.copy(i, 4, line).start()
+
+    def along_far(self, i):
+        for line in self.r.far:
+            self.along(i, line)
+
+    def along_near(self, i):
+        self.along(i, self.r.near[1])
 
     def total(self, i):
         r = self.r
+        self.copy(i, 1, r.z).wait_recv()
+        self.copy(i, 3, r.z).wait_recv()
+        rooms = self.rooms[i]
         value = self.arrays[i][r.z, r.plane].astype(F32)
-        for step in range(1, LINE):
-            value = value + self.last[i][r.behind(step)].astype(F32)
+        value = value + rooms[1][r.z].astype(F32) + rooms[3][r.z].astype(F32)
+        for line in r.far + r.near[1:]:
+            self.got_along(i, line)
+            value = value + rooms[4][line].astype(F32)
         return value
 
-    def finish(self):
+    def sent(self):
         r = self.r
-        for step in range(1, LINE):
-            line = r.behind(step)
-            for i in (0, 1):
-                remote(
-                    self.arrays[i].at[line, r.plane],
-                    self.last[i].at[line],
-                    self.send.at[i, 3, step],
-                    self.recv.at[i, 3, line],
-                    r.at_line(line),
-                ).wait_recv()
-
-    def sent(self):
-        for line in range(LINE):
-            for copy in self.step_one(line) + self.step_two(line):
-                copy.wait_send()
-        for step in range(1, LINE):
-            for copy in self.step_line(step):
-                copy.wait_send()
+        for i in (0, 1):
+            for line in range(LINE):
+                self.copy(i, 1, line).wait_send()
+                self.copy(i, 3, line).wait_send()
+            for line in r.far:
+                self.copy(i, 0, line).wait_send()
+                self.copy(i, 4, line).wait_send()
+            for line in r.near:
+                self.copy(i, 2, line).wait_send()
+            self.copy(i, 4, r.near[1]).wait_send()
 
 
 def loop(count, body):
@@ -752,7 +767,8 @@
     )
     at.gat_s[r.z, r.plane, core] = at.small[...]
     at.gat_s[r.z, r.plane, other] = at.come_s[...]
-    gather_one.start()
+    gather_one.start_line()
+    gather_one.start_sides()
     for chip in range(4 * LINE):
         for which in range(2):
             device = 2 * chip + which
@@ -779,10 +795,15 @@
     for table in (at.near_rows, at.far_rows):
         table[0:256, :] = jnp.zeros((256, 384), BF16)
         table[768:1024, :] = jnp.zeros((256, 384), BF16)
-    for step in range(1, LINE):
-        gather_one.turn(step)
-    gather_one.corner(LINE - 1)
-    gather_two.start()
+    gather_one.round(1)
+    gather_one.corner(0)
+    gather_one.round(2)
+    gather_one.hand(0)
+    gather_one.round(3)
+    gather_one.corner(1)
+    gather_two.start_sides()
+    gather_one.hand(1)
+    gather_two.start_line()
     gather_one.finish()
 
     out_mine = at.gat_b.at[:, :, :, pl.ds(384, 384)]
@@ -823,7 +844,8 @@
     at.near_rows[256:768, :] = low(dot(at.one_hot[...], at.key_rel[...], 0, 0))
     at.far_rows[256:768, :] = low(dot(at.one_hot[...], at.query_rel[...], 0, 0))
 
-    gather_two.turn(1)
+    gather_two.round(1)
+    gather_two.corner(0)
 
     lanes = lax.broadcasted_iota(jnp.int32, (1, 128), 1) // HEAD
     no_score = np.float32(NEGATIVE)
@@ -864,7 +886,17 @@
             here[...] = low(jnp.where(mine, context, here[...].astype(F32)))
 
     def forward_pair(index):
-        loop(2, lambda which: forward_head(2 * index + which))
+        def forward(which):
+            head = 2 * index + which
+            forward_head(head)
+            for after, move in (
+                (1, lambda: gather_two.round(2)),
+                (3, lambda: gather_two.hand(0)),
+                (4, lambda: gather_two.round(3)),
+            ):
+                pl.when(head == after)(move)
+
+        loop(2, forward)
         remote(
             at.context.at[core, :, aligned(index, 128)],
             at.context.at[core, :, aligned(index, 128)],
@@ -874,7 +906,6 @@
         ).start()
 
     loop(3, forward_pair)
-    gather_two.turn(2)
     place_out.wait()
     come_out.wait_recv()
     for index in range(3):
@@ -908,10 +939,10 @@
 
     loop(4, first_norm)
     come_first = swap(10, at.first_low.at[own_rows], at.first_low.at[own_rows])
-    gather_two.turn(3)
+    gather_two.corner(1)
     come_first.wait_recv()
     at.first_turned[...] = at.first_low[...].T
-    gather_two.corner(LINE - 1)
+    gather_two.hand(1)
     gather_two.finish()
 
     def inner_units(index):
@@ -952,24 +983,33 @@
 
     loop(4, second_norm)
     come_grad = swap(12, at.grad_outer.at[own_rows], at.grad_outer.at[own_rows])
-    scatter_two = Scatter(
-        r, (at.grad_1, at.grad_2), (at.one_1, at.one_2), (at.two_1, at.two_2),
-        (at.last_1, at.last_2), at.sf_send, at.sf_recv,
-    )
-    scatter_one = Scatter(
-        r, (at.grad_a, at.grad_b), (at.one_a, at.one_b), (at.two_a, at.two_b),
-        (at.last_a, at.last_b), at.sa_send, at.sa_recv,
-    )
+
+    def scatter(arrays, tags, send, recv):
+        rooms = [[b[kind + tag] for kind in ROOMS] for tag in tags]
+        return Scatter(r, arrays, rooms, send, recv)
+
+    scatter_two = scatter((at.grad_1, at.grad_2), ("1", "2"), at.sf_send, at.sf_recv)
+    scatter_a = scatter((at.grad_o, at.grad_p.at[0]), ("o", "p0"), at.sa_send, at.sa_recv)
+    scatter_b = scatter((at.grad_p.at[1], at.grad_p.at[2]), ("p1", "p2"), at.sb_send, at.sb_recv)
+    scatter_c = scatter((at.grad_t.at[0], at.grad_t.at[1]), ("t0", "t1"), at.sc_send, at.sc_recv)
     come_grad.wait_recv()
 
+    def line_of(index):
+        half = index // 2
+        start = r.pair * (1 - half) + r.z * half
+        return (start + 2 * ((index + 1) // 2 % 2)) % LINE
+
+    def send_lines(i, index, line):
+        pl.when(index < 2)(lambda: scatter_two.begin_far(i, line))
+        pl.when(index >= 2)(lambda: scatter_two.begin_near(i, line))
+
     def outer_weight(index):
-        units = aligned(index, 384)
-        grad = dot(at.active[:, units], at.grad_outer[...], 0, 0)
-        at.grad_2[index] = low(grad).reshape(4, 96, 768)
+        line = line_of(index)
+        grad = dot(at.active[:, aligned(line, 384)], at.grad_outer[...], 0, 0)
+        at.grad_2[line] = low(grad).reshape(4, 96, 768)
+        send_lines(1, index, line)
 
     loop(4, outer_weight)
-    for step in (1, 2, 3, 0):
-        scatter_two.one(step, (1,))
 
     def inner_grad(index):
         units = aligned(index, 384)
@@ -977,11 +1017,16 @@
         pre = low(grad.astype(F32) * at.slope[:, units])
         at.grad_pre[:, units] = pre
         at.bias_inner[0:1, units] = jnp.sum(pre.astype(F32), axis=0, keepdims=True)
-        at.grad_1[:, :, :, units] = low(dot(at.first_turned[...], pre)).reshape(LINE, 4, 48, 384)
 
     loop(4, inner_grad)
-    for step in (1, 2, 3, 0):
-        scatter_two.one(step, (0,))
+
+    def inner_weight(index):
+        line = line_of(index)
+        grad = dot(at.first_turned[aligned(line, 192), :], at.grad_pre[...])
+        at.grad_1[line] = low(grad).reshape(4, 48, 1536)
+        send_lines(0, index, line)
+
+    loop(4, inner_weight)
     at.sums[8:9, :] = at.bias_inner[0:1, 0:768]
     at.sums[9:10, :] = at.bias_inner[0:1, 768:1536]
 
@@ -1011,7 +1056,7 @@
     loop(4, first_norm_back)
     come_att = swap(14, at.grad_att.at[own_rows], at.grad_att.at[own_rows])
     come_att.wait_recv()
-    scatter_two.two(1)
+    scatter_two.corners(1)
     out_rows = pl.ds(pl.multiple_of(2 * core, 2), 2)
     weight_0 = at.out_all[0, out_rows].reshape(384, 384)
     weight_1 = at.out_all[1, out_rows].reshape(384, 384)
@@ -1020,8 +1065,7 @@
     )
     for part in range(2):
         grad = dot(at.context[part], at.grad_att[:, aligned(core, 384)], 0, 0)
-        at.grad_b[2 * part : 2 * part + 2, :, :, 384:768] = low(grad).reshape(2, 4, 48, 384)
-    scatter_two.two(2)
+        at.grad_o[2 * part : 2 * part + 2] = low(grad).reshape(2, 4, 48, 384)
 
     at.near_grad[...] = jnp.zeros_like(at.near_grad)
     at.far_grad[...] = jnp.zeros_like(at.far_grad)
@@ -1072,30 +1116,45 @@
             weights = low(at.soft[head, :, piece])
             merge(at.grad_kvq.at[piece, value_lanes], dot(weights, grad_context, 0, 0))
 
-    def backward_pair(index):
-        loop(2, lambda which: backward_head(2 * index + which))
-        scatter_two.three(index + 1)
-
-        @pl.when(index < 2)
-        def _():
-            scatter_two.two(index + 3)
-
-    loop(3, backward_pair)
-    scatter_two.three(0, True)
-
-    grad_key_rel = dot(at.one_hot[...], low(at.near_grad[256:768, :]))
-    grad_query_rel = dot(at.one_hot[...], low(at.far_grad[256:768, :]))
-    at.key_rel[...] = low(grad_key_rel)
-    at.query_rel[...] = low(grad_query_rel)
-
-    def token_weight(kvq_at):
-        return dot(at.x_turned[...], at.grad_kvq[:, kvq_at : kvq_at + 384])
-
-    def table_weight(rel):
-        return dot(rows(at.table_all[0]), rel[0:256, :]) + dot(rows(at.table_all[1]), rel[256:512, :])
-
     def shape_weight(value):
         return low(value).reshape(LINE, 4, 48, value.shape[-1])
+
+    def weights_pair(index):
+        pair = aligned(index, 128)
+        at.key_rel[:, pair] = low(dot(at.one_hot[...], low(at.near_grad[256:768, pair])))
+        at.query_rel[:, pair] = low(dot(at.one_hot[...], low(at.far_grad[256:768, pair])))
+        for place, rel in enumerate((at.key_rel, None, at.query_rel)):
+            lanes_at = pl.ds(pl.multiple_of(384 * place + index * 128, 128), 128)
+            grad = dot(at.x_turned[...], at.grad_kvq[:, lanes_at])
+            if rel is not None:
+                for part in range(2):
+                    grad = grad + dot(rows(at.table_all[part]), rel[256 * part : 256 * part + 256, pair])
+            at.grad_p[index, :, :, :, 128 * place : 128 * place + 128] = shape_weight(grad)
+
+    def at_step(step, when, *moves):
+        @pl.when(step == when)
+        def _():
+            for move in moves:
+                move()
+
+    def backward_pair(index):
+        def backward(which):
+            head = 2 * index + which
+            backward_head(head)
+            at_step(head, 0, lambda: scatter_two.corners(0))
+            at_step(
+                head, 2, lambda: scatter_two.along_far(1), lambda: scatter_two.along_far(0)
+            )
+            at_step(head, 3, lambda: scatter_two.turn(1))
+            at_step(head, 4, lambda: scatter_two.turn(0), lambda: scatter_a.corners(0))
+
+        loop(2, backward)
+        weights_pair(index)
+        at_step(index, 0, lambda: scatter_a.begin(0), lambda: scatter_a.begin(1))
+        at_step(index, 1, lambda: scatter_b.begin(0))
+        at_step(index, 2, lambda: scatter_b.begin(1))
+
+    loop(3, backward_pair)
 
     def table_half(which):
         piece = aligned(which, 256)
@@ -1105,16 +1164,17 @@
 
     at.table_send[...] = shape_weight(table_half(other))
     come_part = swap(15, at.table_send, at.table_recv)
-    at.grad_a[:, :, :, 0:384] = shape_weight(token_weight(0) + table_weight(at.key_rel))
-    at.grad_a[:, :, :, 384:768] = shape_weight(token_weight(384))
-    for step in (1, 2, 3, 0):
-        scatter_one.one(step, (0,))
-    at.grad_b[:, :, :, 0:384] = shape_weight(token_weight(768) + table_weight(at.query_rel))
     own_table = table_half(core)
+    scatter_two.along_near(1)
     come_part.wait_recv()
-    at.grad_b[:, :, :, 768:1024] = shape_weight(own_table + rows(at.table_recv[...]).astype(F32))
-    for step in (1, 2, 3, 0):
-        scatter_one.one(step, (1,))
+    own_table = own_table + rows(at.table_recv[...]).astype(F32)
+    for part in range(2):
+        at.grad_t[part] = shape_weight(own_table[:, 128 * part : 128 * part + 128])
+        scatter_c.begin(part)
+    scatter_two.along_near(0)
+    scatter_a.corners(1)
+    scatter_b.corners(0)
+    scatter_a.turn(0)
 
     at.sums[0:1, vector_half] = jnp.sum(
         at.grad_kvq[:, 768:1152].astype(F32), axis=0, keepdims=True
@@ -1149,49 +1209,69 @@
     at.sums_step[0] = at.sums[...] + shared
     stage_copies.append(exchange(1, at.sums_step.at[0], r.at_x))
     stage_copies[1].start()
-    scatter_one.two(1)
+    scatter_b.corners(1)
+    scatter_a.along_far(0)
+    scatter_a.turn(1)
+    scatter_b.turn(0)
     input_half(own_rows, at.wide)
-    scatter_one.two(2)
+    for part in range(2):
+        scatter_c.corners(part)
+    scatter_a.along_far(1)
+    scatter_b.along_far(0)
+    scatter_b.turn(1)
     stage_copies[1].wait_recv()
     at.sums_step[1] = at.sums_step[0] + at.sums_come[1]
     stage_copies.append(exchange(2, at.sums_step.at[1], r.at_y))
     stage_copies[2].start()
-    scatter_one.three(1)
-    scatter_one.two(3)
     come_input.wait_recv()
     at.input_grad[...] = low(at.grad_sum[...] + at.wide[...] + at.part_recv[...])
-
-    scatter_two.finish()
-    at.d_outer[...] = scatter_two.total(1)
-    inner_total = scatter_two.total(0)
-    at.give_1[...] = inner_total.reshape(2, 24, 1536)
-    swap(17, at.give_1.at[other], at.d_inner.at[core])
-    at.d_inner[core] = at.give_1[core]
-
-    scatter_one.three(2)
-    scatter_one.two(0)
+    for part in range(2):
+        scatter_a.along_near(part)
+    for part in range(2):
+        scatter_c.turn(part)
+    scatter_b.along_near(0)
+    scatter_b.along_far(1)
+    for part in range(2):
+        scatter_c.along_far(part)
+    scatter_b.along_near(1)
+    for part in range(2):
+        scatter_c.along_near(part)
     stage_copies[2].wait_recv()
     at.sums_step[2] = at.sums_step[1] + at.sums_come[2]
     for step in range(1, LINE):
         copy = exchange(2 + step, at.sums_step.at[2], r.at_line(r.ahead(step)))
         copy.start()
         stage_copies.append(copy)
-    scatter_one.three(3)
-    scatter_one.three(0, True)
+
+    at.d_outer[...] = scatter_two.total(1)
+    at.give_1[...] = scatter_two.total(0).reshape(2, 24, 1536)
+    swap(17, at.give_1.at[other], at.d_inner.at[core])
+    at.d_inner[core] = at.give_1[core]
+    at.give_o[...] = scatter_a.total(0).reshape(2, 24, 384)
+
+    def give_pair(index, total):
+        for place in range(3):
+            start = 384 * place + 128 * index
+            at.give_p[:, :, start : start + 128] = total[:, 128 * place : 128 * place + 128].reshape(
+                2, 24, 128
+            )
+
+    give_pair(0, scatter_a.total(1))
+    give_pair(1, scatter_b.total(0))
+    give_pair(2, scatter_b.total(1))
+    for part in range(2):
+        at.give_t[:, :, 128 * part : 128 * part + 128] = scatter_c.total(part).reshape(2, 24, 128)
     for copy in stage_copies[3:]:
         copy.wait_recv()
     at.vector_grads[...] = (
         at.sums_step[2] + at.sums_come[3] + at.sums_come[4] + at.sums_come[5]
     )
-    scatter_one.finish()
-    at.give_a[...] = scatter_one.total(0).reshape(2, 24, 768)
-    at.give_b[...] = scatter_one.total(1).reshape(2, 24, 1024)
     outs = (
-        (at.give_a, 0, 384, at.d_key),
-        (at.give_a, 384, 384, at.d_value),
-        (at.give_b, 0, 384, at.d_query),
-        (at.give_b, 384, 384, at.d_output),
-        (at.give_b, 768, 256, at.d_table),
+        (at.give_p, 0, 384, at.d_key),
+        (at.give_p, 384, 384, at.d_value),
+        (at.give_p, 768, 384, at.d_query),
+        (at.give_o, 0, 384, at.d_output),
+        (at.give_t, 0, 256, at.d_table),
     )
     for slot, (give, start, width, out) in enumerate(outs):
         swap(18 + slot, give.at[other, :, pl.ds(start, width)], out.at[:, aligned(core, width)])
@@ -1211,7 +1291,7 @@
             at.context_recv.at[index],
             r.partner,
         ).wait_send()
-    for user in (gather_one, gather_two, scatter_two, scatter_one):
+    for user in (gather_one, gather_two, scatter_two, scatter_a, scatter_b, scatter_c):
         user.sent()
 
 
@@ -1341,38 +1421,40 @@
     sums_come=((6, 16, 768), F32),
     grad_1=(BLOCKS + (1536,), BF16),
     grad_2=((LINE, 4, 96, 768), BF16),
-    one_1=((LINE, 2, 48, 1536), BF16),
-    one_2=((LINE, 2, 96, 768), BF16),
-    two_1=((LINE, 48, 1536), BF16),
-    two_2=((LINE, 96, 768), BF16),
-    last_1=((LINE, 48, 1536), BF16),
-    last_2=((LINE, 96, 768), BF16),
-    grad_a=(BLOCKS + (768,), BF16),
-    grad_b=(BLOCKS + (1024,), BF16),
-    one_a=((LINE, 2, 48, 768), BF16),
-    one_b=((LINE, 2, 48, 1024), BF16),
-    two_a=((LINE, 48, 768), BF16),
-    two_b=((LINE, 48, 1024), BF16),
-    last_a=((LINE, 48, 768), BF16),
-    last_b=((LINE, 48, 1024), BF16),
+    grad_o=(BLOCKS + (384,), BF16),
+    grad_p=((3,) + BLOCKS + (384,), BF16),
+    grad_t=((2,) + BLOCKS + (128,), BF16),
     give_1=((2, 24, 1536), F32),
-    give_a=((2, 24, 768), F32),
-    give_b=((2, 24, 1024), F32),
+    give_o=((2, 24, 384), F32),
+    give_p=((2, 24, 1152), F32),
+    give_t=((2, 24, 256), F32),
 )
+ROOMS = dict(pair_=2, first_=LINE, corner_=2, second_=LINE, line_=LINE)
+BLOCK = {
+    "1": (48, 1536), "2": (96, 768), "o": (48, 384), "p0": (48, 384), "p1": (48, 384),
+    "p2": (48, 384), "t0": (48, 128), "t1": (48, 128),
+}
+for tag, block in BLOCK.items():
+    for kind, count in ROOMS.items():
+        SCRATCH[kind + tag] = ((count,) + block, BF16)
 SEMAPHORES = dict(
     swap_send=(23,),
     swap_recv=(23,),
     here=(2,),
     context_send=(3,),
     context_recv=(3,),
-    ga_send=(3, 4, LINE),
-    ga_recv=(3, 4, LINE),
-    gf_send=(2, 4, LINE),
-    gf_recv=(2, 4, LINE),
-    sf_send=(2, 4, LINE),
-    sf_recv=(2, 4, LINE),
-    sa_send=(2, 4, LINE),
-    sa_recv=(2, 4, LINE),
+    ga_send=(3, 6, LINE),
+    ga_recv=(3, 6, LINE),
+    gf_send=(2, 6, LINE),
+    gf_recv=(2, 6, LINE),
+    sf_send=(2, 5, LINE),
+    sf_recv=(2, 5, LINE),
+    sa_send=(2, 5, LINE),
+    sa_recv=(2, 5, LINE),
+    sb_send=(2, 5, LINE),
+    sb_recv=(2, 5, LINE),
+    sc_send=(2, 5, LINE),
+    sc_recv=(2, 5, LINE),
     sums_send=(6,),
     sums_recv=(6,),
 )

time: 200 us -> 182 us (0.910)
  Pallas kernels: 198 us -> 181 us
    pallas_call x1, Pallas kernels: 195 us -> 178 us  [block_shards(): pl.pallas_call(partial(layer_kernel, names), name='layer', out_shape=tupl...]
where the time goes in v3:
time: 182 us
  Pallas kernels  181 us (99%)
    pallas_call x1, Pallas kernels, block_shards(): pl.pallas_call(partial(layer_kernel, names), name='layer', out_shape=tupl...  178 us

profile of v3, /device:TPU:0, one launch (start us, length us, event | category | flops | bytes accessed | tf_op | source)
XLA Modules:
  0.0 182.1 jit_solution(13542211531692135111)
XLA Ops:
  0.7 178.5 %layer.1 = (bf16[256,768]{1,0:T(8,128)(2,1)}, bf16[256,768]{1,0:T(8,128)(2,1)}, f32[24,768]{1,0:T(8,128)}, f32[24,768]{1,0:T(8,128)}, f32[24,768]{1,0:T(8,128)},...) custom-call(bf16[256,768]{1,0:T(8,128)(2,1)} %bitcast.26, ...), custom_call_target="tpu_custom_call" | custom-call | tf_op jit(solution)/shard_map/layer/pallas_call | solution.py:1513
  179.1 2.8 %finish.1 = (bf16[256,768]{1,0:T(8,128)(2,1)}, bf16[256,768]{1,0:T(8,128)(2,1)}, f32[24,768]{1,0:T(8,128)}, f32[24,768]{1,0:T(8,128)}, f32[24,768]{1,0:T(8,128)}...) custom-call(bf16[256,768]{1,0:T(8,128)(2,1)} %get-tuple-element.48.r, ...), custom_call_target="tpu_custom_call" | custom-call | tf_op jit(solution)/shard_map/finish/pallas_call | solution.py:1525

commit v4 on v3

--- a/solution.py
+++ b/solution.py
@@ -426,6 +426,8 @@
         self.pair = self.z + 1 - 2 * (self.z % 2)
         self.near = (self.z, (self.z + 2) % LINE)
         self.far = (self.pair, (self.pair + 2) % LINE)
+        self.soon = 1 + self.z % 2
+        self.late = 3 - 3 * (self.z % 2)
         self.partner = (chip, self.other)
         self.at_x = (self.z * 4 + self.plane_x, self.core)
         self.at_y = (self.z * 4 + self.plane_y, self.core)
@@ -507,13 +509,26 @@
         def _():
             self.got(0, r.z - step)
             self.up(r.z - step)
-            self.sides(r.z - step)
 
         @pl.when(r.z + step < LINE)
         def _():
             self.got(1, r.z + step)
             self.down(r.z + step)
-            self.sides(r.z + step)
+
+    def first(self):
+        self.corner(0)
+        self.round(1)
+        self.sides(self.r.soon)
+
+    def second(self):
+        self.round(2)
+        self.sides(self.r.near[1])
+        self.hand(0)
+
+    def third(self):
+        self.round(3)
+        self.corner(1)
+        self.sides(self.r.late)
 
     def corner(self, which):
         line = self.r.near[which]
@@ -709,6 +724,20 @@
     friends = [r.partner, r.at_x, r.at_y] + [r.at_line(r.ahead(k)) for k in range(1, LINE)]
     for device in friends:
         pl.semaphore_signal(barrier, inc=1, device_id=device, device_id_type=MESH)
+
+    def give_rows(kind, index, array):
+        piece = pl.ds(pl.multiple_of(core * 256 + index * 64, 64), 64)
+        return remote(
+            array.at[piece],
+            array.at[piece],
+            at.row_send.at[kind, index],
+            at.row_recv.at[kind, index],
+            r.partner,
+        )
+
+    def got_rows(kind, array):
+        for index in range(4):
+            give_rows(kind, index, array).wait_recv()
 
     waiting = []
 
@@ -784,23 +813,20 @@
     at.x_turned[...] = at.x_all[...].T
     wide_i = lax.broadcasted_iota(jnp.int32, (512, 512), 0)
     wide_j = lax.broadcasted_iota(jnp.int32, (512, 512), 1)
-    used = low((at.buckets[0:1, 256:768] == wide_i).astype(F32))
-    at.one_hot[...] = low(dot(used, low((wide_i + wide_j == 511).astype(F32))))
+    at.one_natural[...] = low((at.buckets[0:1, 256:768] == wide_i).astype(F32))
+    at.one_hot[...] = low(dot(at.one_natural[...], low((wide_i + wide_j == 511).astype(F32))))
     segment_wide = jnp.broadcast_to(at.segments[...].astype(F32), (128, 512))
     at.segment_row[...] = segment_wide[0:8]
     at.segment_col[...] = segment_wide.T
     flip_i = lax.broadcasted_iota(jnp.int32, (128, 128), 0)
     flip_j = lax.broadcasted_iota(jnp.int32, (128, 128), 1)
     at.flip[...] = low((flip_i + flip_j == 127).astype(F32))
-    for table in (at.near_rows, at.far_rows):
+    for table in (at.near_rows, at.far_rows, at.far_natural):
         table[0:256, :] = jnp.zeros((256, 384), BF16)
         table[768:1024, :] = jnp.zeros((256, 384), BF16)
-    gather_one.round(1)
-    gather_one.corner(0)
-    gather_one.round(2)
-    gather_one.hand(0)
-    gather_one.round(3)
-    gather_one.corner(1)
+    gather_one.first()
+    gather_one.second()
+    gather_one.third()
     gather_two.start_sides()
     gather_one.hand(1)
     gather_two.start_line()
@@ -834,6 +860,7 @@
     at.kvq[:, 0:384] = low(dot(at.x_all[...], rows(at.gat_a[:, :, :, 0:384])))
     at.kvq[:, 384:768] = low(dot(at.x_all[...], rows(at.gat_a[:, :, :, 384:768])) + value_bias)
     at.kvq[:, 768:1152] = low(dot(at.x_all[...], rows(at.gat_b[:, :, :, 0:384])) + query_bias)
+    gather_two.first()
     place_table.wait()
     come_table.wait_recv()
     for part in range(2):
@@ -843,9 +870,7 @@
         at.query_rel[piece, :] = low(dot(table, rows(at.gat_b[:, :, :, 0:384]), 0, 0) + query_bias)
     at.near_rows[256:768, :] = low(dot(at.one_hot[...], at.key_rel[...], 0, 0))
     at.far_rows[256:768, :] = low(dot(at.one_hot[...], at.query_rel[...], 0, 0))
-
-    gather_two.round(1)
-    gather_two.corner(0)
+    at.far_natural[256:768, :] = low(dot(at.one_natural[...], at.query_rel[...], 0, 0))
 
     lanes = lax.broadcasted_iota(jnp.int32, (1, 128), 1) // HEAD
     no_score = np.float32(NEGATIVE)
@@ -880,8 +905,9 @@
             highest = jnp.max(masked, axis=-1, keepdims=True)
             expsum = jnp.exp(masked - highest)
             soft = expsum / jnp.sum(expsum, axis=-1, keepdims=True)
-            at.soft[head, piece, :] = soft
-            context = dot(low(soft), values)
+            rounded = low(soft)
+            at.soft[head, piece, :] = low(dot(at.flip[...], rounded))
+            context = dot(rounded, values)
             here = at.context.at[core, piece, pair]
             here[...] = low(jnp.where(mine, context, here[...].astype(F32)))
 
@@ -889,12 +915,8 @@
         def forward(which):
             head = 2 * index + which
             forward_head(head)
-            for after, move in (
-                (1, lambda: gather_two.round(2)),
-                (3, lambda: gather_two.hand(0)),
-                (4, lambda: gather_two.round(3)),
-            ):
-                pl.when(head == after)(move)
+            pl.when(head == 1)(gather_two.second)
+            pl.when(head == 5)(gather_two.third)
 
         loop(2, forward)
         remote(
@@ -936,11 +958,10 @@
         at.first_normed[piece, :] = normed
         at.first_inverse[piece, :] = jnp.broadcast_to(inverse, (64, 128))
         at.first_low[token_rows, :] = low(out)
+        give_rows(0, index, at.first_low).start()
 
     loop(4, first_norm)
-    come_first = swap(10, at.first_low.at[own_rows], at.first_low.at[own_rows])
-    gather_two.corner(1)
-    come_first.wait_recv()
+    got_rows(0, at.first_low)
     at.first_turned[...] = at.first_low[...].T
     gather_two.hand(1)
     gather_two.finish()
@@ -954,22 +975,25 @@
 
     loop(6, inner_units)
 
-    def outer_half(rows_at, out):
-        for part in range(3):
-            piece = pl.ds(256 * part, 256)
-            out[:, piece] = dot(
-                at.active[rows_at, :], at.gat_2[:, :, :, piece].reshape(1536, 256)
-            )
-
-    outer_half(other_rows, at.part_send)
-    come_outer = swap(11, at.part_send, at.part_recv)
-    outer_half(own_rows, at.wide)
-    come_outer.wait_recv()
+    def outer_part(rows_at, part):
+        return dot(
+            at.active[rows_at, :], at.gat_2[:, :, :, 256 * part : 256 * part + 256].reshape(1536, 256)
+        )
+
+    come_outer = []
+    for part in range(3):
+        piece = pl.ds(256 * part, 256)
+        at.part_send[:, piece] = low(outer_part(other_rows, part))
+        come_outer.append(swap((11, 23, 24)[part], at.part_send.at[:, piece], at.part_recv.at[:, piece]))
+    for part in range(3):
+        at.wide[:, 256 * part : 256 * part + 256] = outer_part(own_rows, part)
+    for copy in come_outer:
+        copy.wait_recv()
 
     def second_norm(index):
         piece = aligned(index, 64)
         token_rows = pl.ds(pl.multiple_of(core * 256 + index * 64, 64), 64)
-        total = at.first_out[piece, :] + at.wide[piece, :] + at.part_recv[piece, :] + vector(5)
+        total = at.first_out[piece, :] + at.wide[piece, :] + at.part_recv[piece, :].astype(F32) + vector(5)
         out, normed, inverse = norm(total, vector(6), vector(7))
         at.result[piece, :] = low(out)
         upstream = at.cotangent[piece, :].astype(F32)
@@ -977,12 +1001,12 @@
         at.grad_sum[piece, :] = grad
         rounded = low(grad)
         at.grad_outer[token_rows, :] = rounded
+        give_rows(1, index, at.grad_outer).start()
         at.sums[5:6, :] += jnp.sum(rounded.astype(F32), axis=0, keepdims=True)
         at.sums[6:7, :] += jnp.sum(upstream * normed, axis=0, keepdims=True)
         at.sums[7:8, :] += jnp.sum(upstream, axis=0, keepdims=True)
 
     loop(4, second_norm)
-    come_grad = swap(12, at.grad_outer.at[own_rows], at.grad_outer.at[own_rows])
 
     def scatter(arrays, tags, send, recv):
         rooms = [[b[kind + tag] for kind in ROOMS] for tag in tags]
@@ -992,7 +1016,18 @@
     scatter_a = scatter((at.grad_o, at.grad_p.at[0]), ("o", "p0"), at.sa_send, at.sa_recv)
     scatter_b = scatter((at.grad_p.at[1], at.grad_p.at[2]), ("p1", "p2"), at.sb_send, at.sb_recv)
     scatter_c = scatter((at.grad_t.at[0], at.grad_t.at[1]), ("t0", "t1"), at.sc_send, at.sc_recv)
-    come_grad.wait_recv()
+
+    def inner_grad(rows_at):
+        for part in range(4):
+            units = pl.ds(384 * part, 384)
+            grad = low(dot(at.grad_outer[rows_at, :], at.gat_2[part].reshape(384, 768), 1, 1))
+            pre = low(grad.astype(F32) * at.slope[rows_at, units])
+            at.grad_pre[rows_at, units] = pre
+            at.bias_inner[0:1, units] += jnp.sum(pre.astype(F32), axis=0, keepdims=True)
+
+    at.bias_inner[...] = jnp.zeros_like(at.bias_inner)
+    inner_grad(own_rows)
+    got_rows(1, at.grad_outer)
 
     def line_of(index):
         half = index // 2
@@ -1011,15 +1046,21 @@
 
     loop(4, outer_weight)
 
-    def inner_grad(index):
-        units = aligned(index, 384)
-        grad = low(dot(at.grad_outer[...], at.gat_2[index].reshape(384, 768), 1, 1))
-        pre = low(grad.astype(F32) * at.slope[:, units])
-        at.grad_pre[:, units] = pre
-        at.bias_inner[0:1, units] = jnp.sum(pre.astype(F32), axis=0, keepdims=True)
-
-    loop(4, inner_grad)
-
+    inner_grad(other_rows)
+    at.sums[8:9, :] = at.bias_inner[0:1, 0:768]
+    at.sums[9:10, :] = at.bias_inner[0:1, 768:1536]
+
+    def first_part(rows_at, part):
+        weight = at.gat_1[2 * part : 2 * part + 2].reshape(384, 1536)
+        return dot(at.grad_pre[rows_at, :], weight, 1, 1)
+
+    come_grad_first = []
+    for part in range(2):
+        piece = pl.ds(384 * part, 384)
+        at.part_send2[:, piece] = low(first_part(other_rows, part))
+        come_grad_first.append(
+            swap((13, 25)[part], at.part_send2.at[:, piece], at.part_recv2.at[:, piece])
+        )
     def inner_weight(index):
         line = line_of(index)
         grad = dot(at.first_turned[aligned(line, 192), :], at.grad_pre[...])
@@ -1027,42 +1068,40 @@
         send_lines(0, index, line)
 
     loop(4, inner_weight)
-    at.sums[8:9, :] = at.bias_inner[0:1, 0:768]
-    at.sums[9:10, :] = at.bias_inner[0:1, 768:1536]
-
-    def first_half(rows_at, out):
-        for part in range(2):
-            weight = at.gat_1[2 * part : 2 * part + 2].reshape(384, 1536)
-            out[:, 384 * part : 384 * part + 384] = dot(at.grad_pre[rows_at, :], weight, 1, 1)
-
-    first_half(other_rows, at.part_send2)
-    come_grad_first = swap(13, at.part_send2, at.part_recv2)
-    first_half(own_rows, at.wide)
-    come_grad_first.wait_recv()
+    for part in range(2):
+        at.wide[:, 384 * part : 384 * part + 384] = first_part(own_rows, part)
+    for copy in come_grad_first:
+        copy.wait_recv()
 
     def first_norm_back(index):
         piece = aligned(index, 64)
         token_rows = pl.ds(pl.multiple_of(core * 256 + index * 64, 64), 64)
-        upstream = at.wide[piece, :] + at.part_recv2[piece, :] + at.grad_sum[piece, :]
+        upstream = at.wide[piece, :] + at.part_recv2[piece, :].astype(F32) + at.grad_sum[piece, :]
         normed = at.first_normed[piece, :]
         grad = norm_pull(upstream, normed, at.first_inverse[piece, 0:1], vector(3))
         at.grad_sum[piece, :] = grad
         rounded = low(grad)
         at.grad_att[token_rows, :] = rounded
+        give_rows(2, index, at.grad_att).start()
         at.sums[2:3, :] += jnp.sum(rounded.astype(F32), axis=0, keepdims=True)
         at.sums[3:4, :] += jnp.sum(upstream * normed, axis=0, keepdims=True)
         at.sums[4:5, :] += jnp.sum(upstream, axis=0, keepdims=True)
 
     loop(4, first_norm_back)
-    come_att = swap(14, at.grad_att.at[own_rows], at.grad_att.at[own_rows])
-    come_att.wait_recv()
+    out_rows = pl.ds(pl.multiple_of(2 * core, 2), 2)
+
+    def context_rows(rows_at):
+        weight_0 = at.out_all[0, out_rows].reshape(384, 384)
+        weight_1 = at.out_all[1, out_rows].reshape(384, 384)
+        at.grad_context[rows_at, :] = low(
+            dot(at.grad_att[rows_at, 0:384], weight_0, 1, 1)
+            + dot(at.grad_att[rows_at, 384:768], weight_1, 1, 1)
+        )
+
+    context_rows(own_rows)
+    got_rows(2, at.grad_att)
+    context_rows(other_rows)
     scatter_two.corners(1)
-    out_rows = pl.ds(pl.multiple_of(2 * core, 2), 2)
-    weight_0 = at.out_all[0, out_rows].reshape(384, 384)
-    weight_1 = at.out_all[1, out_rows].reshape(384, 384)
-    at.grad_context[...] = low(
-        dot(at.grad_att[:, 0:384], weight_0, 1, 1) + dot(at.grad_att[:, 384:768], weight_1, 1, 1)
-    )
     for part in range(2):
         grad = dot(at.context[part], at.grad_att[:, aligned(core, 384)], 0, 0)
         at.grad_o[2 * part : 2 * part + 2] = low(grad).reshape(2, 4, 48, 384)
@@ -1071,65 +1110,92 @@
     at.far_grad[...] = jnp.zeros_like(at.far_grad)
     room = jnp.zeros((128, 128), BF16)
 
-    def spread(flipped):
-        return pltpu.roll(jnp.concatenate([flipped, room], axis=1), 1, 1, stride=1, stride_axis=0)
-
-    def backward_head(head):
-        pair = aligned(head // 2, 128)
-        key_lanes = pl.ds(pl.multiple_of((head // 2) * 128, 128), 128)
-        value_lanes = pl.ds(pl.multiple_of(384 + (head // 2) * 128, 128), 128)
-        query_lanes = pl.ds(pl.multiple_of(768 + (head // 2) * 128, 128), 128)
-        mine = lanes == head % 2
-        only = low(mine.astype(F32))
+    def spread(value, start):
+        wide = jnp.concatenate([value, room], axis=1)
+        return pltpu.roll(wide, start, 1, stride=1, stride_axis=0)
+
+    heads = [low((lanes == which).astype(F32)) for which in range(2)]
+
+    def lanes_of(index, place):
+        return pl.ds(pl.multiple_of(384 * place + index * 128, 128), 128)
+
+    def masked(value):
+        return [value * only for only in heads]
+
+    def backward_queries(index):
+        pair = aligned(index, 128)
         flip = at.flip[...]
-        keys = at.kvq[:, key_lanes]
-        queries = at.kvq[:, query_lanes]
-        values = at.kvq[:, value_lanes]
-
-        def merge(here, value):
-            here[...] = low(jnp.where(mine, value, here[...].astype(F32)))
-
+        keys = masked(at.kvq[:, lanes_of(index, 0)])
+        values = at.kvq[:, lanes_of(index, 1)]
         for block in range(4):
             piece = pl.ds(128 * block, 128)
             window = pl.ds(384 - 128 * block, 640)
-            soft = at.soft[head, piece, :]
-            grad_soft = dot(at.grad_context[piece, pair] * only, values, 1, 1)
-            inner = jnp.sum(soft * grad_soft, axis=-1, keepdims=True)
-            grad_low = low(soft * (grad_soft - inner) * score_scale)
-            at.grad_low[piece, :] = grad_low
-            flipped = low(dot(flip, grad_low))
-            near = spread(flipped)
-            grad = low(dot(flipped, keys) + dot(near, at.near_rows[window, pair]))
-            merge(at.grad_kvq.at[piece, query_lanes], dot(flip, grad))
-            back = low(dot(flip, at.kvq[piece, query_lanes] * only))
-            at.near_grad[window, pair] += dot(near, back, 0, 0)
-        grad_context = at.grad_context[:, pair]
+            back = pl.ds(384 - 128 * block, 128)
+            grad_context = low(dot(flip, at.grad_context[piece, pair]))
+            query = low(dot(flip, at.kvq[piece, lanes_of(index, 2)]))
+            at.turned_grad[piece, :] = grad_context
+            at.turned_query[back, :] = query
+            table = masked(at.near_rows[window, pair])
+            near, grad = [], 0.0
+            for which, context_only in enumerate(masked(grad_context)):
+                soft = at.soft[2 * index + which, piece, :].astype(F32)
+                grad_soft = dot(context_only, values, 1, 1)
+                inner = jnp.sum(soft * grad_soft, axis=-1, keepdims=True)
+                grad_low = low(soft * (grad_soft - inner) * score_scale)
+                at.grad_low[which, back, :] = grad_low
+                near.append(spread(grad_low, 1))
+                grad = grad + dot(grad_low, keys[which]) + dot(near[which], table[which])
+            at.grad_kvq[piece, lanes_of(index, 2)] = low(dot(flip, low(grad)))
+            at.near_grad[window, pair] += dot(
+                jnp.concatenate(near, axis=0), jnp.concatenate(masked(query), axis=0), 0, 0
+            )
+
+    def backward_keys(index):
+        pair = aligned(index, 128)
+        queries = masked(at.turned_query[...])
+        contexts = masked(at.turned_grad[...])
         for block in range(4):
             piece = pl.ds(128 * block, 128)
-            window = pl.ds(384 - 128 * block, 640)
-            flipped = low(dot(flip, at.grad_low[:, piece], 1, 1))
-            far = spread(flipped)
-            grad = low(dot(flipped, queries) + dot(far, at.far_rows[window, pair]))
-            merge(at.grad_kvq.at[piece, key_lanes], dot(flip, grad))
-            back = low(dot(flip, at.kvq[piece, key_lanes] * only))
-            at.far_grad[window, pair] += dot(far, back, 0, 0)
-            weights = low(at.soft[head, :, piece])
-            merge(at.grad_kvq.at[piece, value_lanes], dot(weights, grad_context, 0, 0))
+            window = pl.ds(128 * block, 640)
+            table = masked(at.far_natural[window, pair])
+            far, grad, grad_value = [], 0.0, 0.0
+            for which in range(2):
+                turned = at.grad_low[which, :, piece].T
+                far.append(spread(turned, 0))
+                grad = grad + dot(turned, queries[which]) + dot(far[which], table[which])
+                weights = at.soft[2 * index + which, :, piece]
+                grad_value = grad_value + dot(weights, contexts[which], 0, 0)
+            at.grad_kvq[piece, lanes_of(index, 0)] = low(grad)
+            at.grad_kvq[piece, lanes_of(index, 1)] = low(grad_value)
+            keys = masked(at.kvq[piece, lanes_of(index, 0)])
+            at.far_grad[window, pair] += dot(
+                jnp.concatenate(far, axis=0), jnp.concatenate(keys, axis=0), 0, 0
+            )
 
     def shape_weight(value):
         return low(value).reshape(LINE, 4, 48, value.shape[-1])
 
+    def rel_pair(index):
+        pair = aligned(index, 128)
+        at.key_rel[:, pair] = low(dot(at.one_hot[...], low(at.near_grad[256:768, pair])))
+        at.query_rel[:, pair] = low(dot(at.one_natural[...], low(at.far_grad[256:768, pair])))
+
     def weights_pair(index):
         pair = aligned(index, 128)
-        at.key_rel[:, pair] = low(dot(at.one_hot[...], low(at.near_grad[256:768, pair])))
-        at.query_rel[:, pair] = low(dot(at.one_hot[...], low(at.far_grad[256:768, pair])))
-        for place, rel in enumerate((at.key_rel, None, at.query_rel)):
-            lanes_at = pl.ds(pl.multiple_of(384 * place + index * 128, 128), 128)
-            grad = dot(at.x_turned[...], at.grad_kvq[:, lanes_at])
-            if rel is not None:
-                for part in range(2):
-                    grad = grad + dot(rows(at.table_all[part]), rel[256 * part : 256 * part + 256, pair])
-            at.grad_p[index, :, :, :, 128 * place : 128 * place + 128] = shape_weight(grad)
+        tokens = jnp.concatenate(
+            [at.grad_kvq[:, lanes_of(index, place)] for place in (0, 2, 1)], axis=1
+        )
+        grad = dot(at.x_turned[...], tokens)
+        rel = jnp.concatenate([at.key_rel[:, pair], at.query_rel[:, pair]], axis=1)
+        table = dot(rows(at.table_all[0]), rel[0:256]) + dot(rows(at.table_all[1]), rel[256:512])
+        at.grad_p[index, :, :, :, 0:256] = shape_weight(grad[:, 0:256] + table)
+        at.grad_p[index, :, :, :, 256:384] = shape_weight(grad[:, 256:384])
+
+    def table_half(which):
+        piece = aligned(which, 256)
+        return dot(rows(at.gat_b[:, :, :, 0:384]), at.query_rel[piece, :], 1, 1) + dot(
+            rows(at.gat_a[:, :, :, 0:384]), at.key_rel[piece, :], 1, 1
+        )
 
     def at_step(step, when, *moves):
         @pl.when(step == when)
@@ -1137,35 +1203,34 @@
             for move in moves:
                 move()
 
+    def swap_table():
+        return remote(
+            at.table_send, at.table_recv, at.swap_send.at[15], at.swap_recv.at[15], r.partner
+        )
+
+    def send_table():
+        at.table_send[...] = shape_weight(table_half(other))
+        swap_table().start()
+
     def backward_pair(index):
-        def backward(which):
-            head = 2 * index + which
-            backward_head(head)
-            at_step(head, 0, lambda: scatter_two.corners(0))
-            at_step(
-                head, 2, lambda: scatter_two.along_far(1), lambda: scatter_two.along_far(0)
-            )
-            at_step(head, 3, lambda: scatter_two.turn(1))
-            at_step(head, 4, lambda: scatter_two.turn(0), lambda: scatter_a.corners(0))
-
-        loop(2, backward)
+        backward_queries(index)
+        at_step(index, 0, lambda: scatter_two.corners(0))
+        at_step(index, 1, lambda: scatter_two.along_far(1), lambda: scatter_two.along_far(0))
+        at_step(index, 2, lambda: scatter_two.turn(0), lambda: scatter_a.corners(0))
+        backward_keys(index)
+        rel_pair(index)
+        at_step(index, 2, send_table)
         weights_pair(index)
         at_step(index, 0, lambda: scatter_a.begin(0), lambda: scatter_a.begin(1))
-        at_step(index, 1, lambda: scatter_b.begin(0))
+        at_step(index, 1, lambda: scatter_b.begin(0), lambda: scatter_two.turn(1))
         at_step(index, 2, lambda: scatter_b.begin(1))
 
     loop(3, backward_pair)
 
-    def table_half(which):
-        piece = aligned(which, 256)
-        return dot(rows(at.gat_b[:, :, :, 0:384]), at.query_rel[piece, :], 1, 1) + dot(
-            rows(at.gat_a[:, :, :, 0:384]), at.key_rel[piece, :], 1, 1
-        )
-
-    at.table_send[...] = shape_weight(table_half(other))
-    come_part = swap(15, at.table_send, at.table_recv)
     own_table = table_half(core)
     scatter_two.along_near(1)
+    come_part = swap_table()
+    waiting.append(come_part)
     come_part.wait_recv()
     own_table = own_table + rows(at.table_recv[...]).astype(F32)
     for part in range(2):
@@ -1191,17 +1256,20 @@
     stage_copies = [exchange(0, at.sums, r.partner)]
     stage_copies[0].start()
 
-    def input_half(rows_at, out):
-        for part in range(2):
-            weight_a = at.gat_a[2 * part : 2 * part + 2].reshape(384, 768)
-            weight_b = at.gat_b[2 * part : 2 * part + 2, :, :, 0:384].reshape(384, 384)
-            out[:, 384 * part : 384 * part + 384] = dot(
-                at.grad_kvq[rows_at, 0:768], weight_a, 1, 1
-            ) + dot(at.grad_kvq[rows_at, 768:1152], weight_b, 1, 1)
-
-    come_outer.wait_send()
-    input_half(other_rows, at.part_send)
-    come_input = swap(16, at.part_send, at.part_recv)
+    def input_part(rows_at, part):
+        weight_a = at.gat_a[2 * part : 2 * part + 2].reshape(384, 768)
+        weight_b = at.gat_b[2 * part : 2 * part + 2, :, :, 0:384].reshape(384, 384)
+        return dot(at.grad_kvq[rows_at, 0:768], weight_a, 1, 1) + dot(
+            at.grad_kvq[rows_at, 768:1152], weight_b, 1, 1
+        )
+
+    for copy in come_outer:
+        copy.wait_send()
+    come_input = []
+    for part in range(2):
+        piece = pl.ds(384 * part, 384)
+        at.part_send[:, piece] = low(input_part(other_rows, part))
+        come_input.append(swap((16, 26)[part], at.part_send.at[:, piece], at.part_recv.at[:, piece]))
 
     stage_copies[0].wait_recv()
     lines = lax.broadcasted_iota(jnp.int32, (16, 1), 0)
@@ -1213,7 +1281,8 @@
     scatter_a.along_far(0)
     scatter_a.turn(1)
     scatter_b.turn(0)
-    input_half(own_rows, at.wide)
+    for part in range(2):
+        at.wide[:, 384 * part : 384 * part + 384] = input_part(own_rows, part)
     for part in range(2):
         scatter_c.corners(part)
     scatter_a.along_far(1)
@@ -1223,12 +1292,17 @@
     at.sums_step[1] = at.sums_step[0] + at.sums_come[1]
     stage_copies.append(exchange(2, at.sums_step.at[1], r.at_y))
     stage_copies[2].start()
-    come_input.wait_recv()
-    at.input_grad[...] = low(at.grad_sum[...] + at.wide[...] + at.part_recv[...])
+    for copy in come_input:
+        copy.wait_recv()
+    at.input_grad[...] = low(at.grad_sum[...] + at.wide[...] + at.part_recv[...].astype(F32))
     for part in range(2):
         scatter_a.along_near(part)
     for part in range(2):
         scatter_c.turn(part)
+    at.d_outer[...] = scatter_two.total(1)
+    at.give_1[...] = scatter_two.total(0).reshape(2, 24, 1536)
+    swap(17, at.give_1.at[other], at.d_inner.at[core])
+    at.d_inner[core] = at.give_1[core]
     scatter_b.along_near(0)
     scatter_b.along_far(1)
     for part in range(2):
@@ -1243,10 +1317,6 @@
         copy.start()
         stage_copies.append(copy)
 
-    at.d_outer[...] = scatter_two.total(1)
-    at.give_1[...] = scatter_two.total(0).reshape(2, 24, 1536)
-    swap(17, at.give_1.at[other], at.d_inner.at[core])
-    at.d_inner[core] = at.give_1[core]
     at.give_o[...] = scatter_a.total(0).reshape(2, 24, 384)
 
     def give_pair(index, total):
@@ -1268,21 +1338,24 @@
     )
     outs = (
         (at.give_p, 0, 384, at.d_key),
-        (at.give_p, 384, 384, at.d_value),
-        (at.give_p, 768, 384, at.d_query),
+        (at.give_p, 384, 384, at.d_query),
+        (at.give_p, 768, 384, at.d_value),
         (at.give_o, 0, 384, at.d_output),
         (at.give_t, 0, 256, at.d_table),
     )
     for slot, (give, start, width, out) in enumerate(outs):
         swap(18 + slot, give.at[other, :, pl.ds(start, width)], out.at[:, aligned(core, width)])
         out[:, aligned(core, width)] = give[core, :, start : start + width]
-    for copy in waiting[17:]:
+    for copy in waiting[-6:]:
         copy.wait_recv()
     for copy in waiting:
-        if copy is not come_outer:
+        if all(copy is not early for early in come_outer):
             copy.wait_send()
     for copy in stage_copies:
         copy.wait_send()
+    for kind, array in enumerate((at.first_low, at.grad_outer, at.grad_att)):
+        for index in range(4):
+            give_rows(kind, index, array).wait_send()
     for index in range(3):
         remote(
             at.context.at[core, :, pl.ds(128 * index, 128)],
@@ -1382,6 +1455,8 @@
     flip=((128, 128), BF16),
     near_rows=((1024, 384), BF16),
     far_rows=((1024, 384), BF16),
+    far_natural=((1024, 384), BF16),
+    one_natural=((512, 512), BF16),
     near_grad=((1024, 384), F32),
     far_grad=((1024, 384), F32),
     key_rel=((512, 384), BF16),
@@ -1394,8 +1469,10 @@
     kvq=((512, 1152), BF16),
     grad_kvq=((512, 1152), BF16),
     far_scores=((512, 512), F32),
-    grad_low=((512, 512), BF16),
-    soft=((6, 512, 512), F32),
+    grad_low=((2, 512, 512), BF16),
+    turned_query=((512, 128), BF16),
+    turned_grad=((512, 128), BF16),
+    soft=((6, 512, 512), BF16),
     context=((2, 512, 384), BF16),
     grad_context=((512, 384), BF16),
     wide=((256, 768), F32),
@@ -1407,10 +1484,10 @@
     active=((512, 1536), BF16),
     slope=((512, 1536), F32),
     grad_pre=((512, 1536), BF16),
-    part_send=((256, 768), F32),
-    part_recv=((256, 768), F32),
-    part_send2=((256, 768), F32),
-    part_recv2=((256, 768), F32),
+    part_send=((256, 768), BF16),
+    part_recv=((256, 768), BF16),
+    part_send2=((256, 768), BF16),
+    part_recv2=((256, 768), BF16),
     grad_sum=((256, 768), F32),
     grad_outer=((512, 768), BF16),
     grad_att=((512, 768), BF16),
@@ -1438,8 +1515,10 @@
     for kind, count in ROOMS.items():
         SCRATCH[kind + tag] = ((count,) + block, BF16)
 SEMAPHORES = dict(
-    swap_send=(23,),
-    swap_recv=(23,),
+    swap_send=(27,),
+    swap_recv=(27,),
+    row_send=(3, 4),
+    row_recv=(3, 4),
     here=(2,),
     context_send=(3,),
     context_recv=(3,),

time: 182 us -> 163 us (0.90)
  Pallas kernels: 181 us -> 162 us
    pallas_call x1, Pallas kernels: 178 us -> 159 us  [block_shards(): pl.pallas_call(partial(layer_kernel, names), name='layer', out_shape=tupl...]
where the time goes in v4:
time: 163 us
  Pallas kernels  162 us (99%)
    pallas_call x1, Pallas kernels, block_shards(): pl.pallas_call(partial(layer_kernel, names), name='layer', out_shape=tupl...  159 us

profile of v4, /device:TPU:0, one launch (start us, length us, event | category | flops | bytes accessed | tf_op | source)
XLA Modules:
  0.0 162.9 jit_solution(6450460387924265035)
XLA Ops:
  0.7 159.2 %layer.1 = (bf16[256,768]{1,0:T(8,128)(2,1)}, bf16[256,768]{1,0:T(8,128)(2,1)}, f32[24,768]{1,0:T(8,128)}, f32[24,768]{1,0:T(8,128)}, f32[24,768]{1,0:T(8,128)},...) custom-call(bf16[256,768]{1,0:T(8,128)(2,1)} %bitcast.26, ...), custom_call_target="tpu_custom_call" | custom-call | tf_op jit(solution)/shard_map/layer/pallas_call | solution.py:1592
  159.9 2.8 %finish.1 = (bf16[256,768]{1,0:T(8,128)(2,1)}, bf16[256,768]{1,0:T(8,128)(2,1)}, f32[24,768]{1,0:T(8,128)}, f32[24,768]{1,0:T(8,128)}, f32[24,768]{1,0:T(8,128)}...) custom-call(bf16[256,768]{1,0:T(8,128)(2,1)} %get-tuple-element.48.r, ...), custom_call_target="tpu_custom_call" | custom-call | tf_op jit(solution)/shard_map/finish/pallas_call | solution.py:1604

commit v5 on v4

--- a/solution.py
+++ b/solution.py
@@ -1102,6 +1102,7 @@
     got_rows(2, at.grad_att)
     context_rows(other_rows)
     scatter_two.corners(1)
+    scatter_two.along_far(1)
     for part in range(2):
         grad = dot(at.context[part], at.grad_att[:, aligned(core, 384)], 0, 0)
         at.grad_o[2 * part : 2 * part + 2] = low(grad).reshape(2, 4, 48, 384)
@@ -1214,21 +1215,23 @@
 
     def backward_pair(index):
         backward_queries(index)
+        at_step(index, 2, lambda: scatter_two.turn(0), lambda: scatter_two.turn(1))
+        backward_keys(index)
         at_step(index, 0, lambda: scatter_two.corners(0))
-        at_step(index, 1, lambda: scatter_two.along_far(1), lambda: scatter_two.along_far(0))
-        at_step(index, 2, lambda: scatter_two.turn(0), lambda: scatter_a.corners(0))
-        backward_keys(index)
+        at_step(index, 1, lambda: scatter_a.corners(0), lambda: scatter_two.along_far(0))
+        at_step(index, 2, lambda: scatter_a.along_far(0))
         rel_pair(index)
         at_step(index, 2, send_table)
         weights_pair(index)
         at_step(index, 0, lambda: scatter_a.begin(0), lambda: scatter_a.begin(1))
-        at_step(index, 1, lambda: scatter_b.begin(0), lambda: scatter_two.turn(1))
+        at_step(index, 1, lambda: scatter_b.begin(0), lambda: scatter_a.corners(1))
         at_step(index, 2, lambda: scatter_b.begin(1))
 
     loop(3, backward_pair)
+    scatter_b.corners(0)
+    scatter_a.along_far(1)
 
     own_table = table_half(core)
-    scatter_two.along_near(1)
     come_part = swap_table()
     waiting.append(come_part)
     come_part.wait_recv()
@@ -1236,9 +1239,6 @@
     for part in range(2):
         at.grad_t[part] = shape_weight(own_table[:, 128 * part : 128 * part + 128])
         scatter_c.begin(part)
-    scatter_two.along_near(0)
-    scatter_a.corners(1)
-    scatter_b.corners(0)
     scatter_a.turn(0)
 
     at.sums[0:1, vector_half] = jnp.sum(
@@ -1278,38 +1278,31 @@
     stage_copies.append(exchange(1, at.sums_step.at[0], r.at_x))
     stage_copies[1].start()
     scatter_b.corners(1)
-    scatter_a.along_far(0)
     scatter_a.turn(1)
-    scatter_b.turn(0)
+    scatter_b.along_far(0)
     for part in range(2):
         at.wide[:, 384 * part : 384 * part + 384] = input_part(own_rows, part)
+    for copy in come_input:
+        copy.wait_recv()
+    at.input_grad[...] = low(at.grad_sum[...] + at.wide[...] + at.part_recv[...].astype(F32))
     for part in range(2):
         scatter_c.corners(part)
-    scatter_a.along_far(1)
-    scatter_b.along_far(0)
-    scatter_b.turn(1)
+    for part in range(2):
+        scatter_two.along_near(part)
     stage_copies[1].wait_recv()
     at.sums_step[1] = at.sums_step[0] + at.sums_come[1]
     stage_copies.append(exchange(2, at.sums_step.at[1], r.at_y))
     stage_copies[2].start()
-    for copy in come_input:
-        copy.wait_recv()
-    at.input_grad[...] = low(at.grad_sum[...] + at.wide[...] + at.part_recv[...].astype(F32))
-    for part in range(2):
-        scatter_a.along_near(part)
-    for part in range(2):
-        scatter_c.turn(part)
-    at.d_outer[...] = scatter_two.total(1)
     at.give_1[...] = scatter_two.total(0).reshape(2, 24, 1536)
     swap(17, at.give_1.at[other], at.d_inner.at[core])
     at.d_inner[core] = at.give_1[core]
-    scatter_b.along_near(0)
     scatter_b.along_far(1)
-    for part in range(2):
-        scatter_c.along_far(part)
-    scatter_b.along_near(1)
-    for part in range(2):
-        scatter_c.along_near(part)
+    at.d_outer[...] = scatter_two.total(1)
+    scatter_b.turn(0)
+    scatter_c.along_far(0)
+    scatter_a.along_near(0)
+    scatter_c.along_far(1)
+    scatter_a.along_near(1)
     stage_copies[2].wait_recv()
     at.sums_step[2] = at.sums_step[1] + at.sums_come[2]
     for step in range(1, LINE):
@@ -1317,7 +1310,9 @@
         copy.start()
         stage_copies.append(copy)
 
-    at.give_o[...] = scatter_a.total(0).reshape(2, 24, 384)
+    def give(slot, source, start, width, out):
+        swap(slot, source.at[other, :, pl.ds(start, width)], out.at[:, aligned(core, width)])
+        out[:, aligned(core, width)] = source[core, :, start : start + width]
 
     def give_pair(index, total):
         for place in range(3):
@@ -1326,26 +1321,28 @@
                 2, 24, 128
             )
 
+    at.give_o[...] = scatter_a.total(0).reshape(2, 24, 384)
+    give(21, at.give_o, 0, 384, at.d_output)
+    scatter_b.turn(1)
+    for part in range(2):
+        scatter_c.turn(part)
     give_pair(0, scatter_a.total(1))
+    for user in (scatter_b, scatter_c):
+        for part in range(2):
+            user.along_near(part)
     give_pair(1, scatter_b.total(0))
     give_pair(2, scatter_b.total(1))
+    give(18, at.give_p, 0, 384, at.d_key)
+    give(19, at.give_p, 384, 384, at.d_query)
+    give(20, at.give_p, 768, 384, at.d_value)
     for part in range(2):
         at.give_t[:, :, 128 * part : 128 * part + 128] = scatter_c.total(part).reshape(2, 24, 128)
+    give(22, at.give_t, 0, 256, at.d_table)
     for copy in stage_copies[3:]:
         copy.wait_recv()
     at.vector_grads[...] = (
         at.sums_step[2] + at.sums_come[3] + at.sums_come[4] + at.sums_come[5]
     )
-    outs = (
-        (at.give_p, 0, 384, at.d_key),
-        (at.give_p, 384, 384, at.d_query),
-        (at.give_p, 768, 384, at.d_value),
-        (at.give_o, 0, 384, at.d_output),
-        (at.give_t, 0, 256, at.d_table),
-    )
-    for slot, (give, start, width, out) in enumerate(outs):
-        swap(18 + slot, give.at[other, :, pl.ds(start, width)], out.at[:, aligned(core, width)])
-        out[:, aligned(core, width)] = give[core, :, start : start + width]
     for copy in waiting[-6:]:
         copy.wait_recv()
     for copy in waiting:

time: 163 us -> 159 us (0.975)
  Pallas kernels: 162 us -> 157 us
    pallas_call x1, Pallas kernels: 159 us -> 154 us  [block_shards(): pl.pallas_call(partial(layer_kernel, names), name='layer', out_shape=tupl...]
where the time goes in v5:
time: 159 us; the launch traced here: 158 us
  Pallas kernels  157 us (99%)
    pallas_call x1, Pallas kernels, block_shards(): pl.pallas_call(partial(layer_kernel, names), name='layer', out_shape=tupl...  154 us

profile of v5, /device:TPU:0, one launch (start us, length us, event | category | flops | bytes accessed | tf_op | source)
XLA Modules:
  0.0 157.9 jit_solution(3029545208667187220)
XLA Ops:
  0.7 154.2 %layer.1 = (bf16[256,768]{1,0:T(8,128)(2,1)}, bf16[256,768]{1,0:T(8,128)(2,1)}, f32[24,768]{1,0:T(8,128)}, f32[24,768]{1,0:T(8,128)}, f32[24,768]{1,0:T(8,128)},...) custom-call(bf16[256,768]{1,0:T(8,128)(2,1)} %bitcast.26, ...), custom_call_target="tpu_custom_call" | custom-call | tf_op jit(solution)/shard_map/layer/pallas_call | solution.py:1589
  154.9 2.8 %finish.1 = (bf16[256,768]{1,0:T(8,128)(2,1)}, bf16[256,768]{1,0:T(8,128)(2,1)}, f32[24,768]{1,0:T(8,128)}, f32[24,768]{1,0:T(8,128)}, f32[24,768]{1,0:T(8,128)}...) custom-call(bf16[256,768]{1,0:T(8,128)(2,1)} %get-tuple-element.48.r, ...), custom_call_target="tpu_custom_call" | custom-call | tf_op jit(solution)/shard_map/finish/pallas_call | solution.py:1601

commit v6 on v5

--- a/solution.py
+++ b/solution.py
@@ -748,7 +748,12 @@
         return copy
 
     gather_one = Gather(r, (at.gat_a, at.gat_b, at.gat_s), at.ga_send, at.ga_recv)
-    gather_two = Gather(r, (at.gat_1, at.gat_2), at.gf_send, at.gf_recv)
+    def halves(array):
+        width = array.shape[-1] // 2
+        return [array.at[:, :, :, pl.ds(width * part, width)] for part in range(2)]
+
+    gather_two = Gather(r, halves(at.gat_1), at.gf_send, at.gf_recv)
+    gather_three = Gather(r, halves(at.gat_2), at.gg_send, at.gg_recv)
 
     at.sums[...] = jnp.zeros_like(at.sums)
     at.small_wide[...] = jnp.zeros_like(at.small_wide)
@@ -828,8 +833,10 @@
     gather_one.second()
     gather_one.third()
     gather_two.start_sides()
+    gather_three.start_sides()
     gather_one.hand(1)
     gather_two.start_line()
+    gather_three.start_line()
     gather_one.finish()
 
     out_mine = at.gat_b.at[:, :, :, pl.ds(384, 384)]
@@ -871,6 +878,8 @@
     at.near_rows[256:768, :] = low(dot(at.one_hot[...], at.key_rel[...], 0, 0))
     at.far_rows[256:768, :] = low(dot(at.one_hot[...], at.query_rel[...], 0, 0))
     at.far_natural[256:768, :] = low(dot(at.one_natural[...], at.query_rel[...], 0, 0))
+
+    gather_three.first()
 
     lanes = lax.broadcasted_iota(jnp.int32, (1, 128), 1) // HEAD
     no_score = np.float32(NEGATIVE)
@@ -916,7 +925,9 @@
             head = 2 * index + which
             forward_head(head)
             pl.when(head == 1)(gather_two.second)
-            pl.when(head == 5)(gather_two.third)
+            pl.when(head == 2)(gather_three.second)
+            pl.when(head == 4)(gather_two.third)
+            pl.when(head == 5)(gather_three.third)
 
         loop(2, forward)
         remote(
@@ -961,10 +972,11 @@
         give_rows(0, index, at.first_low).start()
 
     loop(4, first_norm)
+    gather_two.hand(1)
     got_rows(0, at.first_low)
     at.first_turned[...] = at.first_low[...].T
-    gather_two.hand(1)
     gather_two.finish()
+    gather_three.hand(1)
 
     def inner_units(index):
         piece = aligned(index, 256)
@@ -974,6 +986,7 @@
         at.slope[:, piece] = slope
 
     loop(6, inner_units)
+    gather_three.finish()
 
     def outer_part(rows_at, part):
         return dot(
@@ -1361,7 +1374,7 @@
             at.context_recv.at[index],
             r.partner,
         ).wait_send()
-    for user in (gather_one, gather_two, scatter_two, scatter_a, scatter_b, scatter_c):
+    for user in (gather_one, gather_two, gather_three, scatter_two, scatter_a, scatter_b, scatter_c):
         user.sent()
 
 
@@ -1523,6 +1536,8 @@
     ga_recv=(3, 6, LINE),
     gf_send=(2, 6, LINE),
     gf_recv=(2, 6, LINE),
+    gg_send=(2, 6, LINE),
+    gg_recv=(2, 6, LINE),
     sf_send=(2, 5, LINE),
     sf_recv=(2, 5, LINE),
     sa_send=(2, 5, LINE),

time: 159 us -> 157 us (0.987)
  no operation moved by 1% of the time
where the time goes in v6:
time: 157 us
  Pallas kernels  156 us (99%)
    pallas_call x1, Pallas kernels, block_shards(): pl.pallas_call(partial(layer_kernel, names), name='layer', out_shape=tupl...  154 us

profile of v6, /device:TPU:0, one launch (start us, length us, event | category | flops | bytes accessed | tf_op | source)
XLA Modules:
  0.0 157.2 jit_solution(15755006956843110175)
XLA Ops:
  0.7 153.5 %layer.1 = (bf16[256,768]{1,0:T(8,128)(2,1)}, bf16[256,768]{1,0:T(8,128)(2,1)}, f32[24,768]{1,0:T(8,128)}, f32[24,768]{1,0:T(8,128)}, f32[24,768]{1,0:T(8,128)},...) custom-call(bf16[256,768]{1,0:T(8,128)(2,1)} %bitcast.26, ...), custom_call_target="tpu_custom_call" | custom-call | tf_op jit(solution)/shard_map/layer/pallas_call | solution.py:1604
  154.2 2.8 %finish.1 = (bf16[256,768]{1,0:T(8,128)(2,1)}, bf16[256,768]{1,0:T(8,128)(2,1)}, f32[24,768]{1,0:T(8,128)}, f32[24,768]{1,0:T(8,128)}, f32[24,768]{1,0:T(8,128)}...) custom-call(bf16[256,768]{1,0:T(8,128)(2,1)} %get-tuple-element.48.r, ...), custom_call_target="tpu_custom_call" | custom-call | tf_op jit(solution)/shard_map/finish/pallas_call | solution.py:1616

commit v7 on v6

--- a/solution.py
+++ b/solution.py
@@ -829,6 +829,8 @@
     for table in (at.near_rows, at.far_rows, at.far_natural):
         table[0:256, :] = jnp.zeros((256, 384), BF16)
         table[768:1024, :] = jnp.zeros((256, 384), BF16)
+    at.near_grad[...] = jnp.zeros_like(at.near_grad)
+    at.far_grad[...] = jnp.zeros_like(at.far_grad)
     gather_one.first()
     gather_one.second()
     gather_one.third()
@@ -1120,8 +1122,6 @@
         grad = dot(at.context[part], at.grad_att[:, aligned(core, 384)], 0, 0)
         at.grad_o[2 * part : 2 * part + 2] = low(grad).reshape(2, 4, 48, 384)
 
-    at.near_grad[...] = jnp.zeros_like(at.near_grad)
-    at.far_grad[...] = jnp.zeros_like(at.far_grad)
     room = jnp.zeros((128, 128), BF16)
 
     def spread(value, start):

time: 157 us -> 157 us (level)
  no operation moved by 1% of the time
where the time goes in v7:
time: 157 us
  Pallas kernels  156 us (99%)
    pallas_call x1, Pallas kernels, block_shards(): pl.pallas_call(partial(layer_kernel, names), name='layer', out_shape=tupl...  153 us

profile of v7, /device:TPU:0, one launch (start us, length us, event | category | flops | bytes accessed | tf_op | source)
XLA Modules:
  0.0 157.0 jit_solution(10312905586625513788)
XLA Ops:
  0.7 153.3 %layer.1 = (bf16[256,768]{1,0:T(8,128)(2,1)}, bf16[256,768]{1,0:T(8,128)(2,1)}, f32[24,768]{1,0:T(8,128)}, f32[24,768]{1,0:T(8,128)}, f32[24,768]{1,0:T(8,128)},...) custom-call(bf16[256,768]{1,0:T(8,128)(2,1)} %bitcast.26, ...), custom_call_target="tpu_custom_call" | custom-call | tf_op jit(solution)/shard_map/layer/pallas_call | solution.py:1604
  154.0 2.8 %finish.1 = (bf16[256,768]{1,0:T(8,128)(2,1)}, bf16[256,768]{1,0:T(8,128)(2,1)}, f32[24,768]{1,0:T(8,128)}, f32[24,768]{1,0:T(8,128)}, f32[24,768]{1,0:T(8,128)}...) custom-call(bf16[256,768]{1,0:T(8,128)(2,1)} %get-tuple-element.48.r, ...), custom_call_target="tpu_custom_call" | custom-call | tf_op jit(solution)/shard_map/finish/pallas_call | solution.py:1616
